TPU v7x, 32 devices: a whole 2x2x4 slice. The times are simulated.
32 devices in a mesh: chan: 16 (over z, x, core), quad: 2 (over y).
Axes of the slice: x: 2, y: 2, z: 4, core: 2. Of those that a mesh axis runs over, the one named last changes fastest.
Arguments:
- voltages: float32 [2, 512, 1, 2, 8416], P('quad', 'chan'), may hold values from -6 to 6
- filter_taps: float32 [8, 32], replicated, may hold values from -0.375 to 0.375
- phases: int32 [32, 512, 1024], P('chan', None, 'quad'), may hold values from 0 to 255
Outputs:
- visibilities: float32 [32, 2, 1024, 1024], P('chan', None, 'quad')
- beam_power: float32 [32, 512, 256], P('chan', 'quad')
All inputs are finite; a program needn't handle non-finite values.
Results may differ from a plain program's by a relative error of at most 0.0001.
Values sent between devices are 32-bit elements; how exact they have to be, the bound alone decides.
No kernel may reach another device: no remote copies, remote signals or barrier semaphores. Data moves between devices by JAX's collectives and lax.ppermute only.
A program may use at most 128 MiB of HBM per device.

v0:
```python
import functools
import math

import jax
import jax.numpy as jnp
import numpy as np
from jax import lax
from jax.experimental import pallas as pl
from jax.experimental.pallas import tpu as pltpu
from jax.sharding import PartitionSpec as P


PHASE_LEVELS = 256
LANES = 128

f32 = jnp.float32
bf16 = jnp.bfloat16
VMEM = pltpu.VMEM
NT = (((1,), (1,)), ((), ()))
NN = (((1,), (0,)), ((), ()))


def split(x):
    hi = x.astype(bf16)
    return hi, (x - hi.astype(f32)).astype(bf16)


def dot3(a, b, dims):
    mm = functools.partial(lax.dot_general, dimension_numbers=dims, preferred_element_type=f32)
    return mm(a[0], b[0]) + (mm(a[0], b[1]) + mm(a[1], b[0]))


SHIFTS = (0, 1, 3, 2)


def partner(me, size, k, sign):
    z, low = me // size, me % size
    at = ((z ^ (z >> 1)) + 4 + sign * SHIFTS[k // size]) % 4
    return (at ^ (at >> 1)) * size + (low ^ (k % size))


def twiddle_table(fine, per_section):
    n = np.arange(LANES) % fine
    ch = np.arange(fine)
    angle = 2.0 * math.pi * (np.outer(ch, n) % fine) / fine
    cos, sin = np.cos(angle), np.sin(angle)
    table = np.stack([np.stack([cos, -sin], 1), np.stack([sin, cos], 1)], 0)
    table = table.reshape(2, fine // per_section, per_section * 2, LANES)
    return np.ascontiguousarray(table.transpose(1, 0, 2, 3)).astype(np.float32)


def filter_kernel(geom, where, x_ref, table_ref, taps_ref, *rest):
    dishes, coarse, sections, rows4, u_count, j_count, spec_rows, row_count, n = geom
    outs, (coef, coef_hi, coef_lo) = rest[:-3], rest[-3:]
    me = where[0]
    size = n // 4
    chunk = n if coarse == 1 else size
    half = chunk * rows4
    for k in range(n):
        top, kc = k // chunk * u_count * half, k % chunk
        for i in range(2):
            base = table_ref[partner(me, size, k, 1) % sections, i]
            for u in range(u_count):
                for j in range(j_count):
                    c = i * j_count + j
                    row = u * j_count + j
                    coef[top + u * half + kc * rows4 : top + u * half + (kc + 1) * rows4, c * LANES : (c + 1) * LANES] = (
                        base * taps_ref[row : row + 1, :]
                    )
    coef_hi[...], coef_lo[...] = split(coef[...])

    group = u_count
    lane = lax.broadcasted_iota(jnp.int32, (8, LANES), 1)
    sub = lax.broadcasted_iota(jnp.int32, (8, LANES), 0)
    low_lane, low_sub = lane < spec_rows, sub < 4
    for kb in range(n // chunk):
        band = partner(me, size, kb * chunk, 1) // sections if coarse > 1 else 0
        mine = slice(kb * u_count * half, (kb + 1) * u_count * half)

        def step(dg, carry):
            pieces = []
            for d in range(group):
                start = ((dg * group + d) * coarse + band) * row_count * 2
                pieces.append(
                    jnp.concatenate(
                        [
                            x_ref[pl.ds(start + j * 2 + i, spec_rows, stride=2), :]
                            for i in range(2)
                            for j in range(j_count)
                        ],
                        axis=1,
                    )
                )
            x = split(jnp.concatenate(pieces, axis=0))
            out = dot3((coef_hi[mine, :], coef_lo[mine, :]), x, NT)
            per_tile = 8 // rows4
            for g in range(half // 8):
                for u1 in range(2):
                    tiles = []
                    for d1 in range(2):
                        a0, a1 = (
                            out[
                                (u1 * 2 + u0) * half + g * 8 : (u1 * 2 + u0) * half + g * 8 + 8,
                                d1 * LANES : (d1 + 1) * LANES,
                            ]
                            for u0 in range(2)
                        )
                        tiles.append(jnp.where(low_lane, a0, pltpu.roll(a1, spec_rows, 1)))
                        tiles.append(jnp.where(low_lane, pltpu.roll(a0, spec_rows, 1), a1))
                    for t in range(0, group, per_tile):
                        at = pl.multiple_of((dg * group + t) * rows4, 8)
                        for kk in range(per_tile):
                            k = kb * chunk + per_tile * g + kk
                            if per_tile == 2:
                                b0, b1 = tiles[t], tiles[t + 1]
                                if kk == 0:
                                    tile = jnp.where(low_sub, b0, pltpu.roll(b1, 4, 0))
                                else:
                                    tile = jnp.where(low_sub, pltpu.roll(b0, 4, 0), b1)
                            else:
                                tile = jnp.concatenate(
                                    [b[kk * rows4 : (kk + 1) * rows4] for b in tiles[t : t + per_tile]], axis=0
                                )
                            outs[k][u1, pl.ds(at, 8), :] = tile
            return carry

        lax.fori_loop(0, dishes // group, step, 0)


def rows_kernel(samples, x_ref, out_ref):
    full, tail = samples // LANES, samples % LANES

    def step(d, carry):
        for r in range(full):
            out_ref[d, :, r] = x_ref[0, d, :, :, r * LANES : (r + 1) * LANES]
        if tail:
            out_ref[d, :, full] = jnp.zeros(out_ref.shape[1:2] + out_ref.shape[3:], f32)
            out_ref[d, :, full, :, :tail] = x_ref[0, d, :, :, full * LANES :]
        return carry

    lax.fori_loop(0, x_ref.shape[1], step, 0)


def filter_bank(where, voltages, filter_taps, n):
    _, dishes, coarse, parts, samples = voltages.shape
    taps, fine = filter_taps.shape
    spectra = samples // fine - taps + 1
    per_section = coarse * fine // n
    sections = fine // per_section
    u_count = LANES // fine
    j_count = -(-(u_count - 1 + taps) * fine // LANES)
    spec_rows = spectra // u_count
    row_count = spec_rows + j_count - 1
    rows4 = per_section * 2
    assert u_count == 4 and spec_rows == 64 and rows4 in (2, 4) and dishes % 4 == 0
    x = pl.pallas_call(
        functools.partial(rows_kernel, samples),
        in_specs=[pl.BlockSpec(memory_space=VMEM)],
        out_specs=pl.BlockSpec(memory_space=VMEM),
        out_shape=jax.ShapeDtypeStruct((dishes, coarse, row_count, parts, LANES), f32),
        compiler_params=pltpu.CompilerParams(vmem_limit_bytes=1 << 20),
        cost_estimate=pl.CostEstimate(flops=0, bytes_accessed=4 << 20, transcendentals=0),
        name="rows",
    )(voltages)
    x = x.reshape(dishes * coarse * row_count * parts, LANES)
    flat = filter_taps.reshape(-1)
    shifted = [
        jnp.pad(flat, (u * fine, j_count * LANES - taps * fine - u * fine)) for u in range(u_count)
    ]
    taps_rows = jnp.stack(shifted).reshape(u_count * j_count, LANES)
    geom = (dishes, coarse, sections, rows4, u_count, j_count, spec_rows, row_count, n)
    width = 2 * j_count * LANES
    rows = u_count * n * rows4
    block = jax.ShapeDtypeStruct((spectra // LANES, dishes * rows4, LANES), f32)
    return pl.pallas_call(
        functools.partial(filter_kernel, geom),
        grid_spec=pltpu.PrefetchScalarGridSpec(
            num_scalar_prefetch=1,
            grid=(1,),
            in_specs=[pl.BlockSpec(memory_space=VMEM)] * 3,
            out_specs=[pl.BlockSpec(memory_space=VMEM)] * n,
            scratch_shapes=[VMEM((rows, width), f32), VMEM((rows, width), bf16), VMEM((rows, width), bf16)],
        ),
        out_shape=[block] * n,
        compiler_params=pltpu.CompilerParams(vmem_limit_bytes=12 << 20),
        cost_estimate=pl.CostEstimate(
            flops=6 * rows * width * dishes * spec_rows, bytes_accessed=5 << 20, transcendentals=0
        ),
        name="filter_bank",
    )(where, x, jnp.asarray(twiddle_table(fine, per_section)), taps_rows)


def gain_kernel(where, phase_ref, hi_ref, lo_ref):
    beams = phase_ref.shape[1]
    level = phase_ref[0]
    quarter = PHASE_LEVELS // 4
    turn = (level + quarter // 2) // quarter
    x = (level - turn * quarter).astype(f32) * (2.0 * math.pi / PHASE_LEVELS)
    x2 = x * x
    sin = x + x * x2 * (-1.0 / 6 + x2 * (1.0 / 120 + x2 * (-1.0 / 5040 + x2 * (1.0 / 362880))))
    cos = 1.0 + x2 * (-0.5 + x2 * (1.0 / 24 + x2 * (-1.0 / 720 + x2 * (1.0 / 40320 - x2 * (1.0 / 3628800)))))
    odd = (turn & 1) == 1
    c = jnp.where(odd, sin, cos)
    s = jnp.where(odd, cos, sin)
    c = jnp.where(((turn + 1) & 2) == 2, -c, c)
    s = jnp.where((turn & 2) == 2, -s, s)
    hi_ref[0, :beams], lo_ref[0, :beams] = split(c)
    hi_ref[0, beams:], lo_ref[0, beams:] = split(s)


def gains(where, phases, beams, local):
    channels, _, dishes = phases.shape
    out = jax.ShapeDtypeStruct((channels, 2 * beams, dishes), bf16)
    whole = pl.BlockSpec((1, 2 * beams, dishes), lambda p, w: (p, 0, 0))
    return pl.pallas_call(
        gain_kernel,
        grid_spec=pltpu.PrefetchScalarGridSpec(
            num_scalar_prefetch=1,
            grid=(channels,),
            in_specs=[pl.BlockSpec((1, beams, dishes), lambda p, w: (p, w[1] if local else 0, 0))],
            out_specs=[whole, whole],
        ),
        out_shape=[out, out],
        compiler_params=pltpu.CompilerParams(vmem_limit_bytes=(48 if local else 16) << 20),
        cost_estimate=pl.CostEstimate(
            flops=40 * channels * beams * dishes, bytes_accessed=12 * channels * beams * dishes, transcendentals=0
        ),
    )(where, phases)


def put(hi, lo, p, at, rows, col, value):
    h, l = split(value)
    hi[p, pl.ds(at, rows), col : col + value.shape[1]] = h
    lo[p, pl.ds(at, rows), col : col + value.shape[1]] = l


def unpack(blocks, first, me, base, dishes, hi, lo, full):
    channels, _, width = hi.shape
    spectra = width // 2
    count = len(blocks)
    pair = 1 if dishes % 16 == 0 else 16 // dishes
    assert pair <= 2
    rows = pair * dishes
    flip = (me % 2) == 1
    for b in range(0, count, pair):
        place = ((me ^ (first + b)) % count) // pair * rows
        for p in range(channels):
            for part in range(2):
                for u in range(spectra // LANES):
                    got = [
                        block[u, pl.ds(p * 2 + part, dishes, stride=channels * 2), :] for block in blocks[b : b + pair]
                    ]
                    if pair == 2:
                        got = [jnp.where(flip, got[1], got[0]), jnp.where(flip, got[0], got[1])]
                    value = jnp.concatenate(got, axis=0)
                    col = part * spectra + u * LANES
                    put(hi, lo, p, pl.multiple_of(base + place, rows), rows, col, value)
                    if full is not None:
                        full[p, pl.ds(pl.multiple_of(place, rows), rows), col : col + LANES] = value


def own_group_kernel(geom, group, where, *refs):
    _, dishes = geom
    size = LANES // dishes
    blocks = refs[:size]
    outs = refs[size:] if group % 2 == 0 else refs[size + 2 :]
    hi, lo = outs[:2]
    full = outs[2] if len(outs) > 2 else None
    me = where[0]
    base = group % 2 * LANES
    unpack(blocks, group * size, me, base, dishes, hi, lo, full)


def own_group(geom, where, group, blocks, pair, channels, spectra, send):
    half = jax.ShapeDtypeStruct((channels, 2 * LANES, 2 * spectra), bf16)
    full = jax.ShapeDtypeStruct((channels, LANES, 2 * spectra), f32)
    whole = pl.BlockSpec(memory_space=VMEM)
    out = [half, half] + ([full] if send else [])
    at = 1 + len(blocks)
    return pl.pallas_call(
        functools.partial(own_group_kernel, geom, group),
        grid_spec=pltpu.PrefetchScalarGridSpec(
            num_scalar_prefetch=1,
            grid=(1,),
            in_specs=[whole] * (len(blocks) + len(pair)),
            out_specs=[whole] * len(out),
        ),
        out_shape=out,
        input_output_aliases={at: 0, at + 1: 1} if pair else {},
        compiler_params=pltpu.CompilerParams(vmem_limit_bytes=2 << 20),
        cost_estimate=pl.CostEstimate(flops=1 << 20, bytes_accessed=2 << 20, transcendentals=0),
    )(where, *blocks, *pair)


def turned(x):
    half = x.shape[1] // 2
    return jnp.concatenate([-x[:, half:], x[:, :half]], axis=1)


def beam_terms(g_hi, g_lo, p, ats, x):
    hi, lo = ([g[p, :, pl.ds(pl.multiple_of(at, LANES), LANES)] for at in ats] for g in (g_hi, g_lo))
    left = jnp.concatenate(hi + hi + lo, axis=1)
    right = jnp.concatenate([x[0], x[1], x[0]], axis=0)
    return lax.dot_general(left, right, NN, preferred_element_type=f32)


class Writer:
    def __init__(self, vis, stage, sems, scale):
        self.vis, self.stage, self.sems, self.scale = vis, stage, sems, scale
        self.slots, self.copies = 0, []

    def put(self, p, v, rows, cols, value):
        slot = self.slots
        self.slots += 1
        self.stage[slot] = value * self.scale
        for i, row in enumerate(rows):
            for j, col in enumerate(cols):
                source = self.stage.at[slot, i * LANES : (i + 1) * LANES, j * LANES : (j + 1) * LANES]
                target = self.vis.at[
                    p, v, pl.ds(pl.multiple_of(row, LANES), LANES), pl.ds(pl.multiple_of(col, LANES), LANES)
                ]
                copy = pltpu.make_async_copy(source, target, self.sems.at[len(self.copies)])
                copy.start()
                self.copies.append(copy)

    def wide(self, p, rows, cols, left, right):
        self.put(p, 0, rows, cols, dot3(left, right, NT))
        self.put(p, 1, rows, cols, dot3(left, tuple(turned(r) for r in right), NT))

    def narrow(self, p, rows, cols, left, right):
        both = dot3(left, tuple(jnp.concatenate([r, turned(r)], axis=0) for r in right), NT)
        width = right[0].shape[0]
        self.put(p, 0, rows, cols, both[:, :width])
        self.put(p, 1, rows, cols, both[:, width:])

    def finish(self):
        for copy in self.copies:
            copy.wait()


def places(geom, where):
    n, dishes = geom
    size = LANES // dishes
    at = [partner(where[0], size, g * size, -1) // size * LANES for g in range(4)]
    total = n * dishes
    return at, where[1] * total, (1 - where[1]) * total


def first_kernel(geom, where, *refs):
    own_hi, own_lo, far0, far1, gho, glo, ghf, glf, vis, q_ref, far_hi, far_lo, stage, sems = refs
    channels, _, width = own_hi.shape
    at, here, there = places(geom, where)
    near = at[:2]
    out = Writer(vis, stage, sems, 2.0 / width)
    for p in range(channels):
        for g, far in enumerate((far0, far1)):
            put(far_hi, far_lo, p, g * LANES, LANES, 0, far[p])
        mine, theirs = (own_hi[p], own_lo[p]), (far_hi[p], far_lo[p])
        out.wide(p, near, [here + a for a in near], mine, mine)
        out.wide(p, near, [there + a for a in near], mine, theirs)
        q_ref[p] = beam_terms(gho, glo, p, near, mine) + beam_terms(ghf, glf, p, near, theirs)
    out.finish()


def second_kernel(geom, where, *refs):
    near_hi, near_lo, own_hi, own_lo, far_hi, far_lo, gho, glo, q_in, _, vis, q_ref, stage, sems = refs
    channels, _, width = own_hi.shape
    at, here, there = places(geom, where)
    near, away = at[:2], at[2:]
    out = Writer(vis, stage, sems, 2.0 / width)
    for p in range(channels):
        first, mine, theirs = (near_hi[p], near_lo[p]), (own_hi[p], own_lo[p]), (far_hi[p], far_lo[p])
        out.wide(p, away, [here + a for a in away], mine, mine)
        out.wide(p, away, [here + a for a in near], mine, first)
        out.wide(p, near, [here + a for a in away], first, mine)
        out.wide(p, away, [there + a for a in near], mine, theirs)
        q_ref[p] = q_in[p] + beam_terms(gho, glo, p, away, mine)
    out.finish()


def late_kernel(geom, group, raw, where, *refs):
    n, dishes = geom
    size = LANES // dishes
    got, refs = refs[: size if raw else 1], refs[size if raw else 1 :]
    near_hi, near_lo, own_hi, own_lo, ghf, glf, q_in, _, vis, q_ref, stage, sems = refs[:12]
    hi, lo = refs[12:]
    channels, _, width = own_hi.shape
    at, _, there = places(geom, where)
    col = there + at[group]
    if raw:
        unpack(got, group * size, where[0], 0, dishes, hi, lo, None)
    out = Writer(vis, stage, sems, 2.0 / width)
    for p in range(channels):
        if not raw:
            put(hi, lo, p, 0, LANES, 0, got[0][p])
        x = (hi[p], lo[p])
        out.narrow(p, at[:2], [col], (near_hi[p], near_lo[p]), x)
        out.narrow(p, at[2:], [col], (own_hi[p], own_lo[p]), x)
    for p in range(channels):
        q = q_in[p] + beam_terms(ghf, glf, p, [at[group]], (hi[p], lo[p]))
        if not raw:
            q_ref[p] = q
            continue
        beams, spectra = q.shape[0] // 2, q.shape[1] // 2
        re = q[:beams, :spectra] + q[beams:, spectra:]
        im = q[:beams, spectra:] - q[beams:, :spectra]
        power = (re * re + im * im) * (1.0 / (2 * n * dishes))
        u_count = spectra // 64
        got_at = lax.broadcasted_iota(jnp.int32, (spectra, spectra), 0)
        want_at = lax.broadcasted_iota(jnp.int32, (spectra, spectra), 1)
        pick = ((got_at % 64) * u_count + got_at // 64 == want_at).astype(bf16)
        ordered = jnp.zeros_like(power)
        for _ in range(3):
            piece = power.astype(bf16)
            ordered += lax.dot_general(piece, pick, NN, preferred_element_type=f32)
            power = power - piece.astype(f32)
        q_ref[p] = ordered
    out.finish()


def products(kernel, where, ins, outs, aliases, slots, block, more, flops):
    whole, where_it_is = pl.BlockSpec(memory_space=VMEM), pl.BlockSpec(memory_space=pl.ANY)
    vis_shape = outs[0].shape
    return pl.pallas_call(
        kernel,
        grid_spec=pltpu.PrefetchScalarGridSpec(
            num_scalar_prefetch=1,
            grid=(1,),
            in_specs=[where_it_is if x.shape == vis_shape else whole for x in ins],
            out_specs=[where_it_is] + [whole] * (len(outs) - 1),
            scratch_shapes=[VMEM((slots,) + block, f32), pltpu.SemaphoreType.DMA((4 * slots,))] + more,
        ),
        out_shape=outs,
        input_output_aliases={1 + i: o for i, o in aliases.items()},
        compiler_params=pltpu.CompilerParams(vmem_limit_bytes=16 << 20),
        cost_estimate=pl.CostEstimate(flops=flops, bytes_accessed=4 << 20, transcendentals=0),
    )(where, *ins)


def phase_kernel(where, phases, out, sems):
    channels, beams, _ = out.shape
    pieces = sems.shape[0] // channels
    rows = beams // pieces
    at = (1 - where[1]) * beams
    copies = []
    for p in range(channels):
        for i in range(pieces):
            copies.append(
                pltpu.make_async_copy(
                    phases.at[p, pl.ds(pl.multiple_of(at + i * rows, rows), rows), :],
                    out.at[p, i * rows : (i + 1) * rows, :],
                    sems.at[p * pieces + i],
                )
            )
    for copy in copies:
        copy.start()
    for copy in copies:
        copy.wait()


def per_device(n, n_quad, voltages, filter_taps, phases):
    return whole_step(n, n_quad, voltages, filter_taps, phases)


def whole_step(n, n_quad, voltages, filter_taps, phases):
    dishes = voltages.shape[1]
    channels, beams_all, _ = phases.shape
    beams = beams_all // n_quad
    size = LANES // dishes
    groups = n // size
    assert groups == 4
    geom = (n, dishes)
    me = lax.axis_index("chan").astype(jnp.int32)
    quad = lax.axis_index("quad").astype(jnp.int32)
    where = jnp.stack([me, quad])
    swap = [(0, 1), (1, 0)]

    theirs = pl.pallas_call(
        phase_kernel,
        grid_spec=pltpu.PrefetchScalarGridSpec(
            num_scalar_prefetch=1,
            grid=(1,),
            in_specs=[pl.BlockSpec(memory_space=pltpu.HBM)],
            out_specs=pl.BlockSpec(memory_space=VMEM),
            scratch_shapes=[pltpu.SemaphoreType.DMA((8 * channels,))],
        ),
        out_shape=jax.ShapeDtypeStruct((channels, beams, phases.shape[2]), jnp.int32),
        compiler_params=pltpu.CompilerParams(vmem_limit_bytes=60 << 20),
        cost_estimate=pl.CostEstimate(flops=0, bytes_accessed=2 << 20, transcendentals=0),
        name="phase_pick",
    )(where, phases)
    received = lax.ppermute(theirs, "quad", swap)

    sent = filter_bank(where, voltages, filter_taps, n)
    spectra = sent[0].shape[0] * LANES

    own = []
    for k in range(n):
        route = [(i, partner(i, size, k, 1)) for i in range(n)]
        own.append(lax.ppermute(sent[k], "chan", route) if k else sent[k])

    pairs = {0: [], 1: []}
    far = []
    for g in range(groups):
        last = g == groups - 1
        blocks = own[g * size : (g + 1) * size]
        got = own_group(geom, where, g, blocks, pairs[g // 2], channels, spectra, not last)
        pairs[g // 2] = got[:2]
        if not last:
            far.append(lax.ppermute(got[2], "quad", swap))
    raw = []
    for k in range((groups - 1) * size, n):
        raw.append(lax.ppermute(own[k], "quad", swap))

    own_gains = gains(where, phases, beams, True)
    far_gains = gains(where, received, beams, False)

    total = n * dishes
    vis_shape = jax.ShapeDtypeStruct((channels, 2, total, n_quad * total), f32)
    q_shape = jax.ShapeDtypeStruct((channels, 2 * beams, 2 * spectra), f32)
    p_shape = jax.ShapeDtypeStruct((channels, beams, spectra), f32)
    half = jax.ShapeDtypeStruct((channels, 2 * LANES, 2 * spectra), bf16)
    near, away = pairs[0], pairs[1]
    wide, narrow = (2 * LANES, 2 * LANES), (2 * LANES, LANES)
    unit = channels * 6 * 2 * (2 * LANES) * (2 * LANES) * 2 * spectra
    late = [VMEM((channels, LANES, 2 * spectra), bf16)] * 2

    vis, q, far_hi, far_lo = products(
        functools.partial(first_kernel, geom), where,
        [*near, far[0], far[1], *own_gains, *far_gains],
        [vis_shape, q_shape, half, half], {}, 4 * channels, wide, [], 4 * unit,
    )
    vis, q = products(
        functools.partial(second_kernel, geom), where,
        [*near, *away, far_hi, far_lo, *own_gains, q, vis],
        [vis_shape, q_shape], {8: 1, 9: 0}, 8 * channels, wide, [], 5 * unit,
    )
    vis, q = products(
        functools.partial(late_kernel, geom, 2, False), where,
        [far[2], *near, *away, *far_gains, q, vis],
        [vis_shape, q_shape], {7: 1, 8: 0}, 4 * channels, narrow, late, 2 * unit,
    )
    vis, power = products(
        functools.partial(late_kernel, geom, 3, True), where,
        [*raw, *near, *away, *far_gains, q, vis],
        [vis_shape, p_shape], {size + 7: 0}, 4 * channels, narrow, late, 2 * unit,
    )
    return vis, power


def solution(mesh):
    n, n_quad = mesh.shape["chan"], mesh.shape["quad"]
    assert n_quad == 2 and n & (n - 1) == 0
    return jax.shard_map(
        functools.partial(per_device, n, n_quad),
        mesh=mesh,
        in_specs=(P("quad", "chan", None, None, None), P(), P("chan", None, "quad")),
        out_specs=(P("chan", None, "quad", None), P("chan", "quad", None)),
        check_vma=False,
    )
```

profile of v0, /device:TPU:16, one launch (start us, length us, event | category | flops | bytes accessed | tf_op | source)
XLA Modules:
  0.0 95.2 jit_solution(998467075251859830)
XLA Ops:
  1.2 3.1 %phase_pick.1 = s32[2,256,512]{2,1,0:T(8,128)} custom-call(s32[2]{0:T(128)} %pad_add_fusion.where, s32[2,512,512]{2,1,0:T(8,128)} %phase_ref.1), custom_call_target="tpu_custom_call" | custom-call | bytes 2097152 | tf_op jit(solution)/shard_map/phase_pick/pallas_call | solution.py:478
  4.4 1.6 %collective-permute-start.19 = (s32[2,256,512]{2,1,0:T(8,128)}, s32[2,256,512]{2,1,0:T(8,128)S(1)}, u32[]{:S(2)}, u32[]{:S(2)}) collective-permute-start(s32[2,256,512]{2,1,0:T(8,128)} %phase_pick.1), channel_id=1, source_target_pairs={{0,1},{1,0},{2,3},{3,2},{4,5},{5,4},{6,7},{7,6},{8,9},{9,8},{10,11... | collective-permute-start | bytes 3145736 | tf_op jit(solution)/shard_map/ppermute | solution.py:492
  7.0 5.9 %filter_bank.1 = (f32[2,128,128]{2,1,0:T(8,128)S(1)}, f32[2,128,128]{2,1,0:T(8,128)S(1)}, f32[2,128,128]{2,1,0:T(8,128)S(1)}, f32[2,128,128]{2,1,0:T(8,128)S(1)}...) custom-call(s32[2]{0:T(128)S(1)} %copy-done.2, ...), custom_call_target="tpu_custom_call" | custom-call | flops 2415919104 | bytes 5242880 | tf_op jit(solution)/shard_map/filter_bank/pallas_call | solution.py:175
  16.5 2.8 %collective-permute-done.8.refs_0_ = f32[2,128,128]{2,1,0:T(8,128)S(1)} collective-permute-done((f32[2,128,128]{2,1,0:T(8,128)S(1)}, f32[2,128,128]{2,1,0:T(8,128)S(1)}, u32[]{:S(2)}, u32[]{:S(2)}) %collective-permute-start.8) | collective-permute-done | bytes 131104 | tf_op jit(solution)/shard_map/ppermute | solution.py:500
  19.4 3.2 %collective-permute-start.10 = (f32[2,128,128]{2,1,0:T(8,128)S(1)}, f32[2,128,128]{2,1,0:T(8,128)S(1)}, u32[]{:S(2)}, u32[]{:S(2)}) collective-permute-start(f32[2,128,128]{2,1,0:T(8,128)S(1)} %get-tuple-element.47), channel_id=1, source_target_pairs={{0,12},{2,14},{4,8},{6,10},{8,28},{10,30},{12,24},{14,26},{16,4},{... | collective-permute-start | bytes 393224 | tf_op jit(solution)/shard_map/ppermute | solution.py:500
  23.2 1.8 %collective-permute-start = (f32[2,128,128]{2,1,0:T(8,128)S(1)}, f32[2,128,128]{2,1,0:T(8,128)S(1)}, u32[]{:S(2)}, u32[]{:S(2)}) collective-permute-start(f32[2,128,128]{2,1,0:T(8,128)S(1)} %get-tuple-element.41), channel_id=1, source_target_pairs={{0,24},{2,26},{4,28},{6,30},{8,16},{10,18},{12,20},{14,22},{16,8},... | collective-permute-start | bytes 393224 | tf_op jit(solution)/shard_map/ppermute | solution.py:500
  25.1 5.7 %collective-permute-done.14.refs_3_ = f32[2,128,128]{2,1,0:T(8,128)S(1)} collective-permute-done((f32[2,128,128]{2,1,0:T(8,128)S(1)}, f32[2,128,128]{2,1,0:T(8,128)S(1)}, u32[]{:S(2)}, u32[]{:S(2)}) %collective-permute-start.14) | collective-permute-done | bytes 131104 | tf_op jit(solution)/shard_map/ppermute | solution.py:500
  31.4 3.3 %collective-permute-done.11.refs_3_ = f32[2,128,128]{2,1,0:T(8,128)S(1)} collective-permute-done((f32[2,128,128]{2,1,0:T(8,128)S(1)}, f32[2,128,128]{2,1,0:T(8,128)S(1)}, u32[]{:S(2)}, u32[]{:S(2)}) %collective-permute-start.11) | collective-permute-done | bytes 131104 | tf_op jit(solution)/shard_map/ppermute | solution.py:500
  36.0 1.5 %collective-permute-start.21 = (f32[2,128,512]{2,1,0:T(8,128)S(1)}, f32[2,128,512]{2,1,0:T(8,128)S(1)}, u32[]{:S(2)}, u32[]{:S(2)}) collective-permute-start(f32[2,128,512]{2,1,0:T(8,128)S(1)} %get-tuple-element.68), channel_id=1, source_target_pairs={{0,1},{1,0},{2,3},{3,2},{4,5},{5,4},{6,7},{7,6},{8,9},{9,8},{10,11... | collective-permute-start | bytes 1572872 | tf_op jit(solution)/shard_map/ppermute | solution.py:510
  37.5 2.1 %collective-permute-done.refs_0_ = f32[2,128,128]{2,1,0:T(8,128)S(1)} collective-permute-done((f32[2,128,128]{2,1,0:T(8,128)S(1)}, f32[2,128,128]{2,1,0:T(8,128)S(1)}, u32[]{:S(2)}, u32[]{:S(2)}) %collective-permute-start) | collective-permute-done | bytes 131104 | tf_op jit(solution)/shard_map/ppermute | solution.py:500
  39.6 2.3 %collective-permute-start.15 = (f32[2,128,128]{2,1,0:T(8,128)S(1)}, f32[2,128,128]{2,1,0:T(8,128)S(1)}, u32[]{:S(2)}, u32[]{:S(2)}) collective-permute-start(f32[2,128,128]{2,1,0:T(8,128)S(1)} %get-tuple-element.57), channel_id=1, source_target_pairs={{0,16},{2,18},{4,20},{6,22},{8,0},{10,2},{12,4},{14,6},{16,24},{18... | collective-permute-start | bytes 393224 | tf_op jit(solution)/shard_map/ppermute | solution.py:500
  42.6 3.8 %collective-permute-done.15.refs_0_ = f32[2,128,128]{2,1,0:T(8,128)S(1)} collective-permute-done((f32[2,128,128]{2,1,0:T(8,128)S(1)}, f32[2,128,128]{2,1,0:T(8,128)S(1)}, u32[]{:S(2)}, u32[]{:S(2)}) %collective-permute-start.15) | collective-permute-done | bytes 131104 | tf_op jit(solution)/shard_map/ppermute | solution.py:500
  46.5 2.8 %collective-permute-done.16.refs_1_ = f32[2,128,128]{2,1,0:T(8,128)S(1)} collective-permute-done((f32[2,128,128]{2,1,0:T(8,128)S(1)}, f32[2,128,128]{2,1,0:T(8,128)S(1)}, u32[]{:S(2)}, u32[]{:S(2)}) %collective-permute-start.16) | collective-permute-done | bytes 131104 | tf_op jit(solution)/shard_map/ppermute | solution.py:500
  49.3 4.1 %collective-permute-done.17.refs_2_ = f32[2,128,128]{2,1,0:T(8,128)S(1)} collective-permute-done((f32[2,128,128]{2,1,0:T(8,128)S(1)}, f32[2,128,128]{2,1,0:T(8,128)S(1)}, u32[]{:S(2)}, u32[]{:S(2)}) %collective-permute-start.17) | collective-permute-done | bytes 131104 | tf_op jit(solution)/shard_map/ppermute | solution.py:500
  54.5 2.2 %collective-permute-done.18.refs_3_ = f32[2,128,128]{2,1,0:T(8,128)S(1)} collective-permute-done((f32[2,128,128]{2,1,0:T(8,128)S(1)}, f32[2,128,128]{2,1,0:T(8,128)S(1)}, u32[]{:S(2)}, u32[]{:S(2)}) %collective-permute-start.18) | collective-permute-done | bytes 131104 | tf_op jit(solution)/shard_map/ppermute | solution.py:500
  56.7 2.9 %shard_map.64 = (bf16[2,512,512]{2,1,0:T(8,128)(2,1)S(1)}, bf16[2,512,512]{2,1,0:T(8,128)(2,1)S(1)}) custom-call(s32[2]{0:T(128)S(1)} %copy-done.2, s32[2,512,512]{2,1,0:T(8,128)S(1)} %copy-done), custom_call_target="tpu_custom_call" | custom-call | flops 10485760 | bytes 3145728 | tf_op jit(solution)/shard_map/pallas_call | solution.py:215
  60.2 5.2 %collective-permute-done.4.refs_2_ = f32[2,128,128]{2,1,0:T(8,128)S(1)} collective-permute-done((f32[2,128,128]{2,1,0:T(8,128)S(1)}, f32[2,128,128]{2,1,0:T(8,128)S(1)}, u32[]{:S(2)}, u32[]{:S(2)}) %collective-permute-start.4) | collective-permute-done | bytes 131104 | tf_op jit(solution)/shard_map/ppermute | solution.py:500
  65.9 2.1 %collective-permute-done.6.refs_3_ = f32[2,128,128]{2,1,0:T(8,128)S(1)} collective-permute-done((f32[2,128,128]{2,1,0:T(8,128)S(1)}, f32[2,128,128]{2,1,0:T(8,128)S(1)}, u32[]{:S(2)}, u32[]{:S(2)}) %collective-permute-start.6) | collective-permute-done | bytes 131104 | tf_op jit(solution)/shard_map/ppermute | solution.py:500
  69.2 1.6 %collective-permute-start.3 = (f32[2,128,128]{2,1,0:T(8,128)S(1)}, f32[2,128,128]{2,1,0:T(8,128)S(1)}, u32[]{:S(2)}, u32[]{:S(2)}) collective-permute-start(f32[2,128,128]{2,1,0:T(8,128)S(1)} %collective-permute-done.2.refs_1_), channel_id=1, source_target_pairs={{0,1},{1,0},{2,3},{3,2},{4,5},{5,4},{6,7},{7,6},{8,9},{9,8},{10,11... | collective-permute-start | bytes 393224 | tf_op jit(solution)/shard_map/ppermute | solution.py:513
  70.7 3.0 %shard_map.63 = (bf16[2,512,512]{2,1,0:T(8,128)(2,1)S(1)}, bf16[2,512,512]{2,1,0:T(8,128)(2,1)S(1)}) custom-call(s32[2]{0:T(128)S(1)} %copy-done.2, s32[2,256,512]{2,1,0:T(8,128)S(1)} %collective-permute-done.19.phase_ref), custom_call_target="tpu_custom_call" | custom-call | flops 10485760 | bytes 3145728 | tf_op jit(solution)/shard_map/pallas_call | solution.py:215
  75.9 4.6 %shard_map.65 = (f32[2,2,512,1024]{3,2,1,0:T(8,128)}, f32[2,512,512]{2,1,0:T(8,128)S(1)}, bf16[2,256,512]{2,1,0:T(8,128)(2,1)S(1)}, bf16[2,256,512]{2,1,0:T(8,128)(2,1)S(1)}) custom-call(s32[2]{0:T(128)S(1)} %copy-done.2, bf16[2,256,512]{2,1,0:T(8,128)(2,1)S(1)} %get-tuple-element.55.refs_0_.refs_1_.refs_4_, ...), custom_call_target="tpu_custom_call" | custom-call | flops 3221225472 | bytes 4194304 | tf_op jit(solution)/shard_map/pallas_call | solution.py:424
  80.5 6.4 %shard_map.66 = (f32[2,2,512,1024]{3,2,1,0:T(8,128)}, f32[2,512,512]{2,1,0:T(8,128)S(1)}) custom-call(s32[2]{0:T(128)S(1)} %copy-done.2, bf16[2,256,512]{2,1,0:T(8,128)(2,1)S(1)} %get-tuple-element.55.refs_0_.refs_1_.refs_4_, bf16[2,256,512]{2,1,0:T(8,128)(2,1)S(1)} %get-tuple-element.56.refs_1_.refs_2_.refs_5_, ...), custom_call_target="tpu_custom_call", output_to_operand_aliasing={{1}: (9, {}), {0}: (10, {})} | custom-call | flops 4026531840 | bytes 4194304 | tf_op jit(solution)/shard_map/pallas_call | solution.py:424
  86.8 2.7 %shard_map.67 = (f32[2,2,512,1024]{3,2,1,0:T(8,128)}, f32[2,512,512]{2,1,0:T(8,128)S(1)}) custom-call(s32[2]{0:T(128)S(1)} %copy-done.2, f32[2,128,512]{2,1,0:T(8,128)S(1)} %collective-permute-done.20.refs_0_, bf16[2,256,512]{2,1,0:T(8,128)(2,1)S(1)} %get-tuple-element.55.refs_0_.refs_1_.refs_4_, ...), custom_call_target="tpu_custom_call", output_to_operand_aliasing={{1}: (8, {}), {0}: (9, {})} | custom-call | flops 1610612736 | bytes 4194304 | tf_op jit(solution)/shard_map/pallas_call | solution.py:424
  90.4 4.7 %shard_map.68 = (f32[2,2,512,1024]{3,2,1,0:T(8,128)}, f32[2,256,256]{2,1,0:T(8,128)}) custom-call(s32[2]{0:T(128)S(1)} %copy-done.2, f32[2,128,128]{2,1,0:T(8,128)S(1)} %collective-permute-done.1.refs_0_, f32[2,128,128]{2,1,0:T(8,128)S(1)} %collective-permute-done.3.refs_1_, ...), custom_call_target="tpu_custom_call", output_to_operand_aliasing={{0}: (12, {})} | custom-call | flops 1610612736 | bytes 4194304 | tf_op jit(solution)/shard_map/pallas_call | solution.py:424
  (54 shorter events, 14.9 us)
Async XLA Ops:
  4.4 64.8 %collective-permute-start.19 = (s32[2,256,512]{2,1,0:T(8,128)}, s32[2,256,512]{2,1,0:T(8,128)S(1)}, u32[]{:S(2)}, u32[]{:S(2)}) collective-permute-start(s32[2,256,512]{2,1,0:T(8,128)} %phase_pick.1), channel_id=1, source_target_pairs={{0,1},{1,0},{2,3},{3,2},{4,5},{5,4},{6,7},{7,6},{8,9},{9,8},{10,11... | collective-permute-start | bytes 3145736 | tf_op jit(solution)/shard_map/ppermute | solution.py:492
  12.9 43.7 %copy-start = (s32[2,512,512]{2,1,0:T(8,128)S(1)}, s32[2,512,512]{2,1,0:T(8,128)}, u32[]{:S(2)}) copy-start(s32[2,512,512]{2,1,0:T(8,128)} %phase_ref.1) | copy-start | bytes 6291460
  12.9 6.4 %collective-permute-start.8 = (f32[2,128,128]{2,1,0:T(8,128)S(1)}, f32[2,128,128]{2,1,0:T(8,128)S(1)}, u32[]{:S(2)}, u32[]{:S(2)}) collective-permute-start(f32[2,128,128]{2,1,0:T(8,128)S(1)} %get-tuple-element.45), channel_id=1, source_target_pairs={{0,8},{2,10},{4,12},{6,14},{8,24},{10,26},{12,28},{14,30},{16,0},{... | collective-permute-start | bytes 393224 | tf_op jit(solution)/shard_map/ppermute | solution.py:500
  13.3 6.0 %collective-permute-start.9 = (f32[2,128,128]{2,1,0:T(8,128)S(1)}, f32[2,128,128]{2,1,0:T(8,128)S(1)}, u32[]{:S(2)}, u32[]{:S(2)}) collective-permute-start(f32[2,128,128]{2,1,0:T(8,128)S(1)} %get-tuple-element.46), channel_id=1, source_target_pairs={{0,10},{2,8},{4,14},{6,12},{8,26},{10,24},{12,30},{14,28},{16,2},{... | collective-permute-start | bytes 393224 | tf_op jit(solution)/shard_map/ppermute | solution.py:500
  13.8 8.7 %collective-permute-start.12 = (f32[2,128,128]{2,1,0:T(8,128)S(1)}, f32[2,128,128]{2,1,0:T(8,128)S(1)}, u32[]{:S(2)}, u32[]{:S(2)}) collective-permute-start(f32[2,128,128]{2,1,0:T(8,128)S(1)} %get-tuple-element.50), channel_id=1, source_target_pairs={{0,2},{2,0},{4,6},{6,4},{8,10},{10,8},{12,14},{14,12},{16,18},{18,... | collective-permute-start | bytes 393224 | tf_op jit(solution)/shard_map/ppermute | solution.py:500
  15.0 8.2 %collective-permute-start.13 = (f32[2,128,128]{2,1,0:T(8,128)S(1)}, f32[2,128,128]{2,1,0:T(8,128)S(1)}, u32[]{:S(2)}, u32[]{:S(2)}) collective-permute-start(f32[2,128,128]{2,1,0:T(8,128)S(1)} %get-tuple-element.51), channel_id=1, source_target_pairs={{0,4},{2,6},{4,0},{6,2},{8,12},{10,14},{12,8},{14,10},{16,20},{18,... | collective-permute-start | bytes 393224 | tf_op jit(solution)/shard_map/ppermute | solution.py:500
  19.4 11.4 %collective-permute-start.14 = (f32[2,128,128]{2,1,0:T(8,128)S(1)}, f32[2,128,128]{2,1,0:T(8,128)S(1)}, u32[]{:S(2)}, u32[]{:S(2)}) collective-permute-start(f32[2,128,128]{2,1,0:T(8,128)S(1)} %get-tuple-element.52), channel_id=1, source_target_pairs={{0,6},{2,4},{4,2},{6,0},{8,14},{10,12},{12,10},{14,8},{16,22},{18,... | collective-permute-start | bytes 393224 | tf_op jit(solution)/shard_map/ppermute | solution.py:500
  19.4 12.1 %collective-permute-start.10 = (f32[2,128,128]{2,1,0:T(8,128)S(1)}, f32[2,128,128]{2,1,0:T(8,128)S(1)}, u32[]{:S(2)}, u32[]{:S(2)}) collective-permute-start(f32[2,128,128]{2,1,0:T(8,128)S(1)} %get-tuple-element.47), channel_id=1, source_target_pairs={{0,12},{2,14},{4,8},{6,10},{8,28},{10,30},{12,24},{14,26},{16,4},{... | collective-permute-start | bytes 393224 | tf_op jit(solution)/shard_map/ppermute | solution.py:500
  22.5 12.2 %collective-permute-start.11 = (f32[2,128,128]{2,1,0:T(8,128)S(1)}, f32[2,128,128]{2,1,0:T(8,128)S(1)}, u32[]{:S(2)}, u32[]{:S(2)}) collective-permute-start(f32[2,128,128]{2,1,0:T(8,128)S(1)} %get-tuple-element.48), channel_id=1, source_target_pairs={{0,14},{2,12},{4,10},{6,8},{8,30},{10,28},{12,26},{14,24},{16,6},{... | collective-permute-start | bytes 393224 | tf_op jit(solution)/shard_map/ppermute | solution.py:500
  23.2 16.3 %collective-permute-start = (f32[2,128,128]{2,1,0:T(8,128)S(1)}, f32[2,128,128]{2,1,0:T(8,128)S(1)}, u32[]{:S(2)}, u32[]{:S(2)}) collective-permute-start(f32[2,128,128]{2,1,0:T(8,128)S(1)} %get-tuple-element.41), channel_id=1, source_target_pairs={{0,24},{2,26},{4,28},{6,30},{8,16},{10,18},{12,20},{14,22},{16,8},... | collective-permute-start | bytes 393224 | tf_op jit(solution)/shard_map/ppermute | solution.py:500
  30.7 11.9 %collective-permute-start.2 = (f32[2,128,128]{2,1,0:T(8,128)S(1)}, f32[2,128,128]{2,1,0:T(8,128)S(1)}, u32[]{:S(2)}, u32[]{:S(2)}) collective-permute-start(f32[2,128,128]{2,1,0:T(8,128)S(1)} %get-tuple-element.42), channel_id=1, source_target_pairs={{0,26},{2,24},{4,30},{6,28},{8,18},{10,16},{12,22},{14,20},{16,10}... | collective-permute-start | bytes 393224 | tf_op jit(solution)/shard_map/ppermute | solution.py:500
  35.4 38.4 %collective-permute-start.22 = (f32[2,128,512]{2,1,0:T(8,128)S(1)}, f32[2,128,512]{2,1,0:T(8,128)S(1)}, u32[]{:S(2)}, u32[]{:S(2)}) collective-permute-start(f32[2,128,512]{2,1,0:T(8,128)S(1)} %get-tuple-element.69), channel_id=1, source_target_pairs={{0,1},{1,0},{2,3},{3,2},{4,5},{5,4},{6,7},{7,6},{8,9},{9,8},{10,11... | collective-permute-start | bytes 1572872 | tf_op jit(solution)/shard_map/ppermute | solution.py:510
  36.0 38.4 %collective-permute-start.21 = (f32[2,128,512]{2,1,0:T(8,128)S(1)}, f32[2,128,512]{2,1,0:T(8,128)S(1)}, u32[]{:S(2)}, u32[]{:S(2)}) collective-permute-start(f32[2,128,512]{2,1,0:T(8,128)S(1)} %get-tuple-element.68), channel_id=1, source_target_pairs={{0,1},{1,0},{2,3},{3,2},{4,5},{5,4},{6,7},{7,6},{8,9},{9,8},{10,11... | collective-permute-start | bytes 1572872 | tf_op jit(solution)/shard_map/ppermute | solution.py:510
  39.6 6.9 %collective-permute-start.15 = (f32[2,128,128]{2,1,0:T(8,128)S(1)}, f32[2,128,128]{2,1,0:T(8,128)S(1)}, u32[]{:S(2)}, u32[]{:S(2)}) collective-permute-start(f32[2,128,128]{2,1,0:T(8,128)S(1)} %get-tuple-element.57), channel_id=1, source_target_pairs={{0,16},{2,18},{4,20},{6,22},{8,0},{10,2},{12,4},{14,6},{16,24},{18... | collective-permute-start | bytes 393224 | tf_op jit(solution)/shard_map/ppermute | solution.py:500
  42.6 6.6 %collective-permute-start.16 = (f32[2,128,128]{2,1,0:T(8,128)S(1)}, f32[2,128,128]{2,1,0:T(8,128)S(1)}, u32[]{:S(2)}, u32[]{:S(2)}) collective-permute-start(f32[2,128,128]{2,1,0:T(8,128)S(1)} %get-tuple-element.58), channel_id=1, source_target_pairs={{0,18},{2,16},{4,22},{6,20},{8,2},{10,0},{12,6},{14,4},{16,26},{18... | collective-permute-start | bytes 393224 | tf_op jit(solution)/shard_map/ppermute | solution.py:500
  46.5 6.9 %collective-permute-start.17 = (f32[2,128,128]{2,1,0:T(8,128)S(1)}, f32[2,128,128]{2,1,0:T(8,128)S(1)}, u32[]{:S(2)}, u32[]{:S(2)}) collective-permute-start(f32[2,128,128]{2,1,0:T(8,128)S(1)} %get-tuple-element.59), channel_id=1, source_target_pairs={{0,20},{2,22},{4,16},{6,18},{8,4},{10,6},{12,0},{14,2},{16,28},{18... | collective-permute-start | bytes 393224 | tf_op jit(solution)/shard_map/ppermute | solution.py:500
  49.3 7.4 %collective-permute-start.18 = (f32[2,128,128]{2,1,0:T(8,128)S(1)}, f32[2,128,128]{2,1,0:T(8,128)S(1)}, u32[]{:S(2)}, u32[]{:S(2)}) collective-permute-start(f32[2,128,128]{2,1,0:T(8,128)S(1)} %get-tuple-element.60), channel_id=1, source_target_pairs={{0,22},{2,20},{4,18},{6,16},{8,6},{10,4},{12,2},{14,0},{16,30},{18... | collective-permute-start | bytes 393224 | tf_op jit(solution)/shard_map/ppermute | solution.py:500
  53.4 12.0 %collective-permute-start.4 = (f32[2,128,128]{2,1,0:T(8,128)S(1)}, f32[2,128,128]{2,1,0:T(8,128)S(1)}, u32[]{:S(2)}, u32[]{:S(2)}) collective-permute-start(f32[2,128,128]{2,1,0:T(8,128)S(1)} %get-tuple-element.43), channel_id=1, source_target_pairs={{0,28},{2,30},{4,24},{6,26},{8,20},{10,22},{12,16},{14,18},{16,12}... | collective-permute-start | bytes 393224 | tf_op jit(solution)/shard_map/ppermute | solution.py:500
  56.7 11.3 %collective-permute-start.6 = (f32[2,128,128]{2,1,0:T(8,128)S(1)}, f32[2,128,128]{2,1,0:T(8,128)S(1)}, u32[]{:S(2)}, u32[]{:S(2)}) collective-permute-start(f32[2,128,128]{2,1,0:T(8,128)S(1)} %get-tuple-element.44), channel_id=1, source_target_pairs={{0,30},{2,28},{4,26},{6,24},{8,22},{10,20},{12,18},{14,16},{16,14}... | collective-permute-start | bytes 393224 | tf_op jit(solution)/shard_map/ppermute | solution.py:500
  65.4 21.4 %collective-permute-start.20 = (f32[2,128,512]{2,1,0:T(8,128)S(1)}, f32[2,128,512]{2,1,0:T(8,128)S(1)}, u32[]{:S(2)}, u32[]{:S(2)}) collective-permute-start(f32[2,128,512]{2,1,0:T(8,128)S(1)} %get-tuple-element.67), channel_id=1, source_target_pairs={{0,1},{1,0},{2,3},{3,2},{4,5},{5,4},{6,7},{7,6},{8,9},{9,8},{10,11... | collective-permute-start | bytes 1572872 | tf_op jit(solution)/shard_map/ppermute | solution.py:510
  68.0 21.5 %collective-permute-start.1 = (f32[2,128,128]{2,1,0:T(8,128)S(1)}, f32[2,128,128]{2,1,0:T(8,128)S(1)}, u32[]{:S(2)}, u32[]{:S(2)}) collective-permute-start(f32[2,128,128]{2,1,0:T(8,128)S(1)} %collective-permute-done.refs_0_), channel_id=1, source_target_pairs={{0,1},{1,0},{2,3},{3,2},{4,5},{5,4},{6,7},{7,6},{8,9},{9,8},{10,11... | collective-permute-start | bytes 393224 | tf_op jit(solution)/shard_map/ppermute | solution.py:513
  69.2 20.4 %collective-permute-start.3 = (f32[2,128,128]{2,1,0:T(8,128)S(1)}, f32[2,128,128]{2,1,0:T(8,128)S(1)}, u32[]{:S(2)}, u32[]{:S(2)}) collective-permute-start(f32[2,128,128]{2,1,0:T(8,128)S(1)} %collective-permute-done.2.refs_1_), channel_id=1, source_target_pairs={{0,1},{1,0},{2,3},{3,2},{4,5},{5,4},{6,7},{7,6},{8,9},{9,8},{10,11... | collective-permute-start | bytes 393224 | tf_op jit(solution)/shard_map/ppermute | solution.py:513
  73.8 15.8 %collective-permute-start.5 = (f32[2,128,128]{2,1,0:T(8,128)S(1)}, f32[2,128,128]{2,1,0:T(8,128)S(1)}, u32[]{:S(2)}, u32[]{:S(2)}) collective-permute-start(f32[2,128,128]{2,1,0:T(8,128)S(1)} %collective-permute-done.4.refs_2_), channel_id=1, source_target_pairs={{0,1},{1,0},{2,3},{3,2},{4,5},{5,4},{6,7},{7,6},{8,9},{9,8},{10,11... | collective-permute-start | bytes 393224 | tf_op jit(solution)/shard_map/ppermute | solution.py:513
  74.4 16.0 %collective-permute-start.7 = (f32[2,128,128]{2,1,0:T(8,128)S(1)}, f32[2,128,128]{2,1,0:T(8,128)S(1)}, u32[]{:S(2)}, u32[]{:S(2)}) collective-permute-start(f32[2,128,128]{2,1,0:T(8,128)S(1)} %collective-permute-done.6.refs_3_), channel_id=1, source_target_pairs={{0,1},{1,0},{2,3},{3,2},{4,5},{5,4},{6,7},{7,6},{8,9},{9,8},{10,11... | collective-permute-start | bytes 393224 | tf_op jit(solution)/shard_map/ppermute | solution.py:513
  (4 other events, 12.3 us)
where the time goes:
time: 95.5 us; the launch traced here: 95.2 us
  Pallas kernels  36.1 us (38%)
  waiting for transfers between devices  35.7 us (37%)
  starting transfers between devices  21 us (22%)
  between operations  1.04 us (1%)
    ppermute x15, waiting for transfers between devices, whole_step(): own.append(lax.ppermute(sent[k], 'chan', route) if k else sent[k])  34.9 us
    pallas_call x4, Pallas kernels, products(): pl.pallas_call(kernel, grid_spec=pltpu.PrefetchScalarGridSpec(num_scalar_...  18.3 us
    ppermute x15, starting transfers between devices, whole_step(): own.append(lax.ppermute(sent[k], 'chan', route) if k else sent[k])  12.6 us
    pallas_call x2, Pallas kernels, gains(): pl.pallas_call(gain_kernel, grid_spec=pltpu.PrefetchScalarGridSpec(num_sc...  5.89 us
    pallas_call x1, Pallas kernels, filter_bank(): pl.pallas_call(functools.partial(filter_kernel, geom), grid_spec=pltpu.Pr...  5.88 us
    ppermute x4, starting transfers between devices, whole_step(): raw.append(lax.ppermute(own[k], 'quad', swap))  4.18 us
    pallas_call x1, Pallas kernels, whole_step(): pl.pallas_call(phase_kernel, grid_spec=pltpu.PrefetchScalarGridSpec(num_s...  3.14 us
    pallas_call x4, Pallas kernels, own_group(): pl.pallas_call(functools.partial(own_group_kernel, geom, group), grid_spe...  2.65 us
  transfers between devices with their start and end apart: 23, of which 12 were waited for; matrix products, arithmetic and copies ran while one was open for 0% of the time, Pallas kernels for 30%

commit v1 on v0

--- a/solution.py
+++ b/solution.py
@@ -56,18 +56,33 @@
     size = n // 4
     chunk = n if coarse == 1 else size
     half = chunk * rows4
+    fine = LANES // u_count
+    phase = lax.broadcasted_iota(jnp.int32, (1, LANES), 1) // fine
     for k in range(n):
         top, kc = k // chunk * u_count * half, k % chunk
         for i in range(2):
             base = table_ref[partner(me, size, k, 1) % sections, i]
             for u in range(u_count):
-                for j in range(j_count):
-                    c = i * j_count + j
-                    row = u * j_count + j
-                    coef[top + u * half + kc * rows4 : top + u * half + (kc + 1) * rows4, c * LANES : (c + 1) * LANES] = (
-                        base * taps_ref[row : row + 1, :]
-                    )
+                row = top + u * half + kc * rows4
+                coef[row : row + rows4, i * LANES : (i + 1) * LANES] = jnp.where(phase == u, base, 0.0)
     coef_hi[...], coef_lo[...] = split(coef[...])
+
+    taps = [taps_ref[t : t + 1, :] for t in range(2 * u_count)]
+    weights = []
+    for m in range(u_count):
+        inside = phase >= m
+        first, second = taps[m], taps[u_count + m]
+        weights.append(
+            (jnp.where(inside, first, 0.0), jnp.where(inside, second, first), jnp.where(inside, 0.0, second))
+        )
+
+    def filtered(start):
+        rows = [x_ref[pl.ds(start + 2 * j, spec_rows, stride=2), :] for j in range(j_count)]
+        total = rows[0] * weights[0][0] + rows[1] * weights[0][1]
+        for m in range(1, u_count):
+            part = rows[0] * weights[m][0] + rows[1] * weights[m][1] + rows[2] * weights[m][2]
+            total = total + pltpu.roll(part, LANES - m * fine, 1)
+        return total
 
     group = u_count
     lane = lax.broadcasted_iota(jnp.int32, (8, LANES), 1)
@@ -81,16 +96,7 @@
             pieces = []
             for d in range(group):
                 start = ((dg * group + d) * coarse + band) * row_count * 2
-                pieces.append(
-                    jnp.concatenate(
-                        [
-                            x_ref[pl.ds(start + j * 2 + i, spec_rows, stride=2), :]
-                            for i in range(2)
-                            for j in range(j_count)
-                        ],
-                        axis=1,
-                    )
-                )
+                pieces.append(jnp.concatenate([filtered(start + i) for i in range(2)], axis=1))
             x = split(jnp.concatenate(pieces, axis=0))
             out = dot3((coef_hi[mine, :], coef_lo[mine, :]), x, NT)
             per_tile = 8 // rows4
@@ -124,7 +130,7 @@
                             outs[k][u1, pl.ds(at, 8), :] = tile
             return carry
 
-        lax.fori_loop(0, dishes // group, step, 0)
+        lax.fori_loop(0, dishes // group, step, 0, unroll=2)
 
 
 def rows_kernel(samples, x_ref, out_ref):
@@ -152,7 +158,7 @@
     spec_rows = spectra // u_count
     row_count = spec_rows + j_count - 1
     rows4 = per_section * 2
-    assert u_count == 4 and spec_rows == 64 and rows4 in (2, 4) and dishes % 4 == 0
+    assert u_count == 4 and taps == 8 and j_count == 3 and spec_rows == 64 and rows4 in (2, 4) and dishes % 4 == 0
     x = pl.pallas_call(
         functools.partial(rows_kernel, samples),
         in_specs=[pl.BlockSpec(memory_space=VMEM)],
@@ -163,13 +169,9 @@
         name="rows",
     )(voltages)
     x = x.reshape(dishes * coarse * row_count * parts, LANES)
-    flat = filter_taps.reshape(-1)
-    shifted = [
-        jnp.pad(flat, (u * fine, j_count * LANES - taps * fine - u * fine)) for u in range(u_count)
-    ]
-    taps_rows = jnp.stack(shifted).reshape(u_count * j_count, LANES)
+    taps_rows = jnp.tile(filter_taps, (1, u_count))
     geom = (dishes, coarse, sections, rows4, u_count, j_count, spec_rows, row_count, n)
-    width = 2 * j_count * LANES
+    width = 2 * LANES
     rows = u_count * n * rows4
     block = jax.ShapeDtypeStruct((spectra // LANES, dishes * rows4, LANES), f32)
     return pl.pallas_call(
@@ -190,26 +192,31 @@
     )(where, x, jnp.asarray(twiddle_table(fine, per_section)), taps_rows)
 
 
-def gain_kernel(where, phase_ref, hi_ref, lo_ref):
-    beams = phase_ref.shape[1]
-    level = phase_ref[0]
-    quarter = PHASE_LEVELS // 4
-    turn = (level + quarter // 2) // quarter
-    x = (level - turn * quarter).astype(f32) * (2.0 * math.pi / PHASE_LEVELS)
-    x2 = x * x
-    sin = x + x * x2 * (-1.0 / 6 + x2 * (1.0 / 120 + x2 * (-1.0 / 5040 + x2 * (1.0 / 362880))))
-    cos = 1.0 + x2 * (-0.5 + x2 * (1.0 / 24 + x2 * (-1.0 / 720 + x2 * (1.0 / 40320 - x2 * (1.0 / 3628800)))))
-    odd = (turn & 1) == 1
-    c = jnp.where(odd, sin, cos)
-    s = jnp.where(odd, cos, sin)
-    c = jnp.where(((turn + 1) & 2) == 2, -c, c)
-    s = jnp.where((turn & 2) == 2, -s, s)
-    hi_ref[0, :beams], lo_ref[0, :beams] = split(c)
-    hi_ref[0, beams:], lo_ref[0, beams:] = split(s)
-
-
-def gains(where, phases, beams, local):
-    channels, _, dishes = phases.shape
+def gain_kernel(where, *refs):
+    *pieces, hi_ref, lo_ref = refs
+    beams = hi_ref.shape[1] // 2
+    row = 0
+    for piece in pieces:
+        count = piece.shape[1]
+        level = piece[0]
+        quarter = PHASE_LEVELS // 4
+        turn = (level + quarter // 2) // quarter
+        x = (level - turn * quarter).astype(f32) * (2.0 * math.pi / PHASE_LEVELS)
+        x2 = x * x
+        sin = x + x * x2 * (-1.0 / 6 + x2 * (1.0 / 120 + x2 * (-1.0 / 5040 + x2 * (1.0 / 362880))))
+        cos = 1.0 + x2 * (-0.5 + x2 * (1.0 / 24 + x2 * (-1.0 / 720 + x2 * (1.0 / 40320 - x2 * (1.0 / 3628800)))))
+        odd = (turn & 1) == 1
+        c = jnp.where(odd, sin, cos)
+        s = jnp.where(odd, cos, sin)
+        c = jnp.where(((turn + 1) & 2) == 2, -c, c)
+        s = jnp.where((turn & 2) == 2, -s, s)
+        hi_ref[0, row : row + count], lo_ref[0, row : row + count] = split(c)
+        hi_ref[0, beams + row : beams + row + count], lo_ref[0, beams + row : beams + row + count] = split(s)
+        row += count
+
+
+def gains(where, pieces, beams, local):
+    channels, _, dishes = pieces[0].shape
     out = jax.ShapeDtypeStruct((channels, 2 * beams, dishes), bf16)
     whole = pl.BlockSpec((1, 2 * beams, dishes), lambda p, w: (p, 0, 0))
     return pl.pallas_call(
@@ -217,7 +224,10 @@
         grid_spec=pltpu.PrefetchScalarGridSpec(
             num_scalar_prefetch=1,
             grid=(channels,),
-            in_specs=[pl.BlockSpec((1, beams, dishes), lambda p, w: (p, w[1] if local else 0, 0))],
+            in_specs=[
+                pl.BlockSpec((1, beams if local else x.shape[1], dishes), lambda p, w: (p, w[1] if local else 0, 0))
+                for x in pieces
+            ],
             out_specs=[whole, whole],
         ),
         out_shape=[out, out],
@@ -225,7 +235,7 @@
         cost_estimate=pl.CostEstimate(
             flops=40 * channels * beams * dishes, bytes_accessed=12 * channels * beams * dishes, transcendentals=0
         ),
-    )(where, phases)
+    )(where, *pieces)
 
 
 def put(hi, lo, p, at, rows, col, value):
@@ -259,37 +269,33 @@
                         full[p, pl.ds(pl.multiple_of(place, rows), rows), col : col + LANES] = value
 
 
-def own_group_kernel(geom, group, where, *refs):
+def own_group_kernel(geom, group, *refs):
     _, dishes = geom
     size = LANES // dishes
     blocks = refs[:size]
     outs = refs[size:] if group % 2 == 0 else refs[size + 2 :]
     hi, lo = outs[:2]
     full = outs[2] if len(outs) > 2 else None
-    me = where[0]
+    me = lax.axis_index("chan")
     base = group % 2 * LANES
     unpack(blocks, group * size, me, base, dishes, hi, lo, full)
 
 
-def own_group(geom, where, group, blocks, pair, channels, spectra, send):
+def own_group(geom, group, blocks, pair, channels, spectra, send):
     half = jax.ShapeDtypeStruct((channels, 2 * LANES, 2 * spectra), bf16)
     full = jax.ShapeDtypeStruct((channels, LANES, 2 * spectra), f32)
     whole = pl.BlockSpec(memory_space=VMEM)
     out = [half, half] + ([full] if send else [])
-    at = 1 + len(blocks)
+    at = len(blocks)
     return pl.pallas_call(
         functools.partial(own_group_kernel, geom, group),
-        grid_spec=pltpu.PrefetchScalarGridSpec(
-            num_scalar_prefetch=1,
-            grid=(1,),
-            in_specs=[whole] * (len(blocks) + len(pair)),
-            out_specs=[whole] * len(out),
-        ),
+        in_specs=[whole] * (len(blocks) + len(pair)),
+        out_specs=[whole] * len(out),
         out_shape=out,
         input_output_aliases={at: 0, at + 1: 1} if pair else {},
         compiler_params=pltpu.CompilerParams(vmem_limit_bytes=2 << 20),
         cost_estimate=pl.CostEstimate(flops=1 << 20, bytes_accessed=2 << 20, transcendentals=0),
-    )(where, *blocks, *pair)
+    )(*blocks, *pair)
 
 
 def turned(x):
@@ -338,18 +344,19 @@
             copy.wait()
 
 
-def places(geom, where):
+def places(geom):
     n, dishes = geom
     size = LANES // dishes
-    at = [partner(where[0], size, g * size, -1) // size * LANES for g in range(4)]
+    me, quad = lax.axis_index("chan"), lax.axis_index("quad")
+    at = [partner(me, size, g * size, -1) // size * LANES for g in range(4)]
     total = n * dishes
-    return at, where[1] * total, (1 - where[1]) * total
-
-
-def first_kernel(geom, where, *refs):
+    return at, quad * total, (1 - quad) * total
+
+
+def first_kernel(geom, *refs):
     own_hi, own_lo, far0, far1, gho, glo, ghf, glf, vis, q_ref, far_hi, far_lo, stage, sems = refs
     channels, _, width = own_hi.shape
-    at, here, there = places(geom, where)
+    at, here, there = places(geom)
     near = at[:2]
     out = Writer(vis, stage, sems, 2.0 / width)
     for p in range(channels):
@@ -362,10 +369,10 @@
     out.finish()
 
 
-def second_kernel(geom, where, *refs):
+def second_kernel(geom, *refs):
     near_hi, near_lo, own_hi, own_lo, far_hi, far_lo, gho, glo, q_in, _, vis, q_ref, stage, sems = refs
     channels, _, width = own_hi.shape
-    at, here, there = places(geom, where)
+    at, here, there = places(geom)
     near, away = at[:2], at[2:]
     out = Writer(vis, stage, sems, 2.0 / width)
     for p in range(channels):
@@ -378,29 +385,27 @@
     out.finish()
 
 
-def late_kernel(geom, group, raw, where, *refs):
+def late_kernel(geom, group, raw, *refs):
     n, dishes = geom
     size = LANES // dishes
     got, refs = refs[: size if raw else 1], refs[size if raw else 1 :]
     near_hi, near_lo, own_hi, own_lo, ghf, glf, q_in, _, vis, q_ref, stage, sems = refs[:12]
-    hi, lo = refs[12:]
+    hi, lo, *more = refs[12:]
     channels, _, width = own_hi.shape
-    at, _, there = places(geom, where)
+    at, _, there = places(geom)
     col = there + at[group]
     if raw:
-        unpack(got, group * size, where[0], 0, dishes, hi, lo, None)
+        unpack(got, group * size, lax.axis_index("chan"), 0, dishes, hi, lo, None)
     out = Writer(vis, stage, sems, 2.0 / width)
+    copies = []
     for p in range(channels):
         if not raw:
             put(hi, lo, p, 0, LANES, 0, got[0][p])
-        x = (hi[p], lo[p])
-        out.narrow(p, at[:2], [col], (near_hi[p], near_lo[p]), x)
-        out.narrow(p, at[2:], [col], (own_hi[p], own_lo[p]), x)
-    for p in range(channels):
         q = q_in[p] + beam_terms(ghf, glf, p, [at[group]], (hi[p], lo[p]))
         if not raw:
             q_ref[p] = q
             continue
+        held, held_sems = more
         beams, spectra = q.shape[0] // 2, q.shape[1] // 2
         re = q[:beams, :spectra] + q[beams:, spectra:]
         im = q[:beams, spectra:] - q[beams:, :spectra]
@@ -414,34 +419,39 @@
             piece = power.astype(bf16)
             ordered += lax.dot_general(piece, pick, NN, preferred_element_type=f32)
             power = power - piece.astype(f32)
-        q_ref[p] = ordered
+        held[p] = ordered
+        copy = pltpu.make_async_copy(held.at[p], q_ref.at[p], held_sems.at[p])
+        copy.start()
+        copies.append(copy)
+    for p in range(channels):
+        x = (hi[p], lo[p])
+        out.narrow(p, at[:2], [col], (near_hi[p], near_lo[p]), x)
+        out.narrow(p, at[2:], [col], (own_hi[p], own_lo[p]), x)
+    for copy in copies:
+        copy.wait()
     out.finish()
 
 
-def products(kernel, where, ins, outs, aliases, slots, block, more, flops):
+def products(kernel, ins, outs, aliases, slots, block, more, flops, last=False):
     whole, where_it_is = pl.BlockSpec(memory_space=VMEM), pl.BlockSpec(memory_space=pl.ANY)
     vis_shape = outs[0].shape
     return pl.pallas_call(
         kernel,
-        grid_spec=pltpu.PrefetchScalarGridSpec(
-            num_scalar_prefetch=1,
-            grid=(1,),
-            in_specs=[where_it_is if x.shape == vis_shape else whole for x in ins],
-            out_specs=[where_it_is] + [whole] * (len(outs) - 1),
-            scratch_shapes=[VMEM((slots,) + block, f32), pltpu.SemaphoreType.DMA((4 * slots,))] + more,
-        ),
+        in_specs=[where_it_is if x.shape == vis_shape else whole for x in ins],
+        out_specs=[where_it_is] + [where_it_is if x.dtype == f32 and last else whole for x in outs[1:]],
+        scratch_shapes=[VMEM((slots,) + block, f32), pltpu.SemaphoreType.DMA((4 * slots,))] + more,
         out_shape=outs,
-        input_output_aliases={1 + i: o for i, o in aliases.items()},
+        input_output_aliases=aliases,
         compiler_params=pltpu.CompilerParams(vmem_limit_bytes=16 << 20),
         cost_estimate=pl.CostEstimate(flops=flops, bytes_accessed=4 << 20, transcendentals=0),
-    )(where, *ins)
-
-
-def phase_kernel(where, phases, out, sems):
-    channels, beams, _ = out.shape
+    )(*ins)
+
+
+def phase_kernel(beams, first, phases, out, sems):
+    channels, count, _ = out.shape
     pieces = sems.shape[0] // channels
-    rows = beams // pieces
-    at = (1 - where[1]) * beams
+    rows = count // pieces
+    at = (1 - lax.axis_index("quad")) * beams + first
     copies = []
     for p in range(channels):
         for i in range(pieces):
@@ -458,6 +468,20 @@
         copy.wait()
 
 
+def phase_piece(phases, beams, first, count):
+    channels, _, dishes = phases.shape
+    pieces = count // 32
+    return pl.pallas_call(
+        functools.partial(phase_kernel, beams, first),
+        in_specs=[pl.BlockSpec(memory_space=pltpu.HBM)],
+        out_specs=pl.BlockSpec(memory_space=VMEM),
+        scratch_shapes=[pltpu.SemaphoreType.DMA((pieces * channels,))],
+        out_shape=jax.ShapeDtypeStruct((channels, count, dishes), jnp.int32),
+        compiler_params=pltpu.CompilerParams(vmem_limit_bytes=60 << 20),
+        cost_estimate=pl.CostEstimate(flops=0, bytes_accessed=2 << 20, transcendentals=0),
+    )(phases)
+
+
 def per_device(n, n_quad, voltages, filter_taps, phases):
     return whole_step(n, n_quad, voltages, filter_taps, phases)
 
@@ -475,21 +499,10 @@
     where = jnp.stack([me, quad])
     swap = [(0, 1), (1, 0)]
 
-    theirs = pl.pallas_call(
-        phase_kernel,
-        grid_spec=pltpu.PrefetchScalarGridSpec(
-            num_scalar_prefetch=1,
-            grid=(1,),
-            in_specs=[pl.BlockSpec(memory_space=pltpu.HBM)],
-            out_specs=pl.BlockSpec(memory_space=VMEM),
-            scratch_shapes=[pltpu.SemaphoreType.DMA((8 * channels,))],
-        ),
-        out_shape=jax.ShapeDtypeStruct((channels, beams, phases.shape[2]), jnp.int32),
-        compiler_params=pltpu.CompilerParams(vmem_limit_bytes=60 << 20),
-        cost_estimate=pl.CostEstimate(flops=0, bytes_accessed=2 << 20, transcendentals=0),
-        name="phase_pick",
-    )(where, phases)
-    received = lax.ppermute(theirs, "quad", swap)
+    received = []
+    for first, count in ((0, beams),):
+        piece = phase_piece(phases, beams, first, count)
+        received.append(lax.ppermute(piece, "quad", swap))
 
     sent = filter_bank(where, voltages, filter_taps, n)
     spectra = sent[0].shape[0] * LANES
@@ -504,7 +517,7 @@
     for g in range(groups):
         last = g == groups - 1
         blocks = own[g * size : (g + 1) * size]
-        got = own_group(geom, where, g, blocks, pairs[g // 2], channels, spectra, not last)
+        got = own_group(geom, g, blocks, pairs[g // 2], channels, spectra, not last)
         pairs[g // 2] = got[:2]
         if not last:
             far.append(lax.ppermute(got[2], "quad", swap))
@@ -512,7 +525,7 @@
     for k in range((groups - 1) * size, n):
         raw.append(lax.ppermute(own[k], "quad", swap))
 
-    own_gains = gains(where, phases, beams, True)
+    own_gains = gains(where, [phases], beams, True)
     far_gains = gains(where, received, beams, False)
 
     total = n * dishes
@@ -524,26 +537,27 @@
     wide, narrow = (2 * LANES, 2 * LANES), (2 * LANES, LANES)
     unit = channels * 6 * 2 * (2 * LANES) * (2 * LANES) * 2 * spectra
     late = [VMEM((channels, LANES, 2 * spectra), bf16)] * 2
+    power = [VMEM((channels, beams, spectra), f32), pltpu.SemaphoreType.DMA((channels,))]
 
     vis, q, far_hi, far_lo = products(
-        functools.partial(first_kernel, geom), where,
+        functools.partial(first_kernel, geom),
         [*near, far[0], far[1], *own_gains, *far_gains],
         [vis_shape, q_shape, half, half], {}, 4 * channels, wide, [], 4 * unit,
     )
     vis, q = products(
-        functools.partial(second_kernel, geom), where,
+        functools.partial(second_kernel, geom),
         [*near, *away, far_hi, far_lo, *own_gains, q, vis],
         [vis_shape, q_shape], {8: 1, 9: 0}, 8 * channels, wide, [], 5 * unit,
     )
     vis, q = products(
-        functools.partial(late_kernel, geom, 2, False), where,
+        functools.partial(late_kernel, geom, 2, False),
         [far[2], *near, *away, *far_gains, q, vis],
         [vis_shape, q_shape], {7: 1, 8: 0}, 4 * channels, narrow, late, 2 * unit,
     )
     vis, power = products(
-        functools.partial(late_kernel, geom, 3, True), where,
+        functools.partial(late_kernel, geom, 3, True),
         [*raw, *near, *away, *far_gains, q, vis],
-        [vis_shape, p_shape], {size + 7: 0}, 4 * channels, narrow, late, 2 * unit,
+        [vis_shape, p_shape], {size + 7: 0}, 4 * channels, narrow, late + power, 2 * unit, True,
     )
     return vis, power
 

time: 95.5 us -> 91.9 us (0.962)
  Pallas kernels: 36.1 us -> 30.2 us
  waiting for transfers between devices: 35.7 us -> 39.3 us
    pallas_call x9, Pallas kernels: 24.1 us -> 19.4 us  [the longest x4 16.4 us: products(): pl.pallas_call(kernel, in_specs=[where_it_is if x.shape == vis_shape else...]
    ppermute x15, waiting for transfers between devices: 34.9 us -> 36.9 us  [whole_step(): own.append(lax.ppermute(sent[k], 'chan', route) if k else sent[k])]
    ppermute x4, waiting for transfers between devices: 0.83 us -> 2.4 us  [whole_step(): raw.append(lax.ppermute(own[k], 'quad', swap))]
    pallas_call x1, Pallas kernels: 5.88 us -> 4.65 us  [filter_bank(): pl.pallas_call(functools.partial(filter_kernel, geom), grid_spec=pltpu.Pr...]
  transfers between devices with their start and end apart: 23 -> 23, of which waited for: 12 -> 13; matrix products, arithmetic and copies ran while one was open for 0% -> 0% of each run, Pallas kernels for 30% -> 26%
where the time goes in v1:
time: 91.9 us; the launch traced here: 91.8 us
  waiting for transfers between devices  39.3 us (43%)
  Pallas kernels  30.2 us (33%)
  starting transfers between devices  20.6 us (22%)
  between operations  0.96 us (1%)
    ppermute x15, waiting for transfers between devices, whole_step(): own.append(lax.ppermute(sent[k], 'chan', route) if k else sent[k])  36.9 us
    pallas_call x4, Pallas kernels, products(): pl.pallas_call(kernel, in_specs=[where_it_is if x.shape == vis_shape else...  16.4 us
    ppermute x15, starting transfers between devices, whole_step(): own.append(lax.ppermute(sent[k], 'chan', route) if k else sent[k])  12.3 us
    pallas_call x2, Pallas kernels, gains(): pl.pallas_call(gain_kernel, grid_spec=pltpu.PrefetchScalarGridSpec(num_sc...  5.89 us
    pallas_call x1, Pallas kernels, filter_bank(): pl.pallas_call(functools.partial(filter_kernel, geom), grid_spec=pltpu.Pr...  4.65 us
    ppermute x4, starting transfers between devices, whole_step(): raw.append(lax.ppermute(own[k], 'quad', swap))  4.18 us
    ppermute x3, starting transfers between devices, whole_step(): far.append(lax.ppermute(got[2], 'quad', swap))  2.59 us
    pallas_call x1, Pallas kernels, phase_piece(): pl.pallas_call(functools.partial(phase_kernel, beams, first), in_specs=[p...  2.5 us
  transfers between devices with their start and end apart: 23, of which 13 were waited for; matrix products, arithmetic and copies ran while one was open for 0% of the time, Pallas kernels for 26%

profile of v1, /device:TPU:16, one launch (start us, length us, event | category | flops | bytes accessed | tf_op | source)
XLA Modules:
  0.0 91.8 jit_solution(14765684621302413056)
XLA Ops:
  0.6 2.5 %shard_map.63 = s32[2,256,512]{2,1,0:T(8,128)} custom-call(s32[2,512,512]{2,1,0:T(8,128)} %refs_0_.1), custom_call_target="tpu_custom_call" | custom-call | bytes 2097152 | tf_op jit(solution)/shard_map/pallas_call | solution.py:474
  3.2 1.6 %collective-permute-start.19 = (s32[2,256,512]{2,1,0:T(8,128)}, s32[2,256,512]{2,1,0:T(8,128)S(1)}, u32[]{:S(2)}, u32[]{:S(2)}) collective-permute-start(s32[2,256,512]{2,1,0:T(8,128)} %shard_map.63), channel_id=1, source_target_pairs={{0,1},{1,0},{2,3},{3,2},{4,5},{5,4},{6,7},{7,6},{8,9},{9,8},{10,11... | collective-permute-start | bytes 3145736 | tf_op jit(solution)/shard_map/ppermute | solution.py:505
  5.7 4.6 %filter_bank.1 = (f32[2,128,128]{2,1,0:T(8,128)S(1)}, f32[2,128,128]{2,1,0:T(8,128)S(1)}, f32[2,128,128]{2,1,0:T(8,128)S(1)}, f32[2,128,128]{2,1,0:T(8,128)S(1)}...) custom-call(s32[2]{0:T(128)S(1)} %pad_add_fusion.where, ...), custom_call_target="tpu_custom_call" | custom-call | flops 805306368 | bytes 5242880 | tf_op jit(solution)/shard_map/filter_bank/pallas_call | solution.py:177
  13.9 2.8 %collective-permute-done.8.refs_0_ = f32[2,128,128]{2,1,0:T(8,128)S(1)} collective-permute-done((f32[2,128,128]{2,1,0:T(8,128)S(1)}, f32[2,128,128]{2,1,0:T(8,128)S(1)}, u32[]{:S(2)}, u32[]{:S(2)}) %collective-permute-start.8) | collective-permute-done | bytes 131104 | tf_op jit(solution)/shard_map/ppermute | solution.py:513
  16.7 3.2 %collective-permute-start.10 = (f32[2,128,128]{2,1,0:T(8,128)S(1)}, f32[2,128,128]{2,1,0:T(8,128)S(1)}, u32[]{:S(2)}, u32[]{:S(2)}) collective-permute-start(f32[2,128,128]{2,1,0:T(8,128)S(1)} %get-tuple-element.47), channel_id=1, source_target_pairs={{0,12},{2,14},{4,8},{6,10},{8,28},{10,30},{12,24},{14,26},{16,4},{... | collective-permute-start | bytes 393224 | tf_op jit(solution)/shard_map/ppermute | solution.py:513
  20.6 1.8 %collective-permute-start = (f32[2,128,128]{2,1,0:T(8,128)S(1)}, f32[2,128,128]{2,1,0:T(8,128)S(1)}, u32[]{:S(2)}, u32[]{:S(2)}) collective-permute-start(f32[2,128,128]{2,1,0:T(8,128)S(1)} %get-tuple-element.41), channel_id=1, source_target_pairs={{0,24},{2,26},{4,28},{6,30},{8,16},{10,18},{12,20},{14,22},{16,8},... | collective-permute-start | bytes 393224 | tf_op jit(solution)/shard_map/ppermute | solution.py:513
  22.5 5.7 %collective-permute-done.14.refs_3_ = f32[2,128,128]{2,1,0:T(8,128)S(1)} collective-permute-done((f32[2,128,128]{2,1,0:T(8,128)S(1)}, f32[2,128,128]{2,1,0:T(8,128)S(1)}, u32[]{:S(2)}, u32[]{:S(2)}) %collective-permute-start.14) | collective-permute-done | bytes 131104 | tf_op jit(solution)/shard_map/ppermute | solution.py:513
  28.3 3.8 %collective-permute-done.11.refs_3_ = f32[2,128,128]{2,1,0:T(8,128)S(1)} collective-permute-done((f32[2,128,128]{2,1,0:T(8,128)S(1)}, f32[2,128,128]{2,1,0:T(8,128)S(1)}, u32[]{:S(2)}, u32[]{:S(2)}) %collective-permute-start.11) | collective-permute-done | bytes 131104 | tf_op jit(solution)/shard_map/ppermute | solution.py:513
  34.3 2.6 %collective-permute-done.refs_0_ = f32[2,128,128]{2,1,0:T(8,128)S(1)} collective-permute-done((f32[2,128,128]{2,1,0:T(8,128)S(1)}, f32[2,128,128]{2,1,0:T(8,128)S(1)}, u32[]{:S(2)}, u32[]{:S(2)}) %collective-permute-start) | collective-permute-done | bytes 131104 | tf_op jit(solution)/shard_map/ppermute | solution.py:513
  37.0 1.7 %collective-permute-start.15 = (f32[2,128,128]{2,1,0:T(8,128)S(1)}, f32[2,128,128]{2,1,0:T(8,128)S(1)}, u32[]{:S(2)}, u32[]{:S(2)}) collective-permute-start(f32[2,128,128]{2,1,0:T(8,128)S(1)} %get-tuple-element.57), channel_id=1, source_target_pairs={{0,16},{2,18},{4,20},{6,22},{8,0},{10,2},{12,4},{14,6},{16,24},{18... | collective-permute-start | bytes 393224 | tf_op jit(solution)/shard_map/ppermute | solution.py:513
  40.0 3.8 %collective-permute-done.15.refs_0_ = f32[2,128,128]{2,1,0:T(8,128)S(1)} collective-permute-done((f32[2,128,128]{2,1,0:T(8,128)S(1)}, f32[2,128,128]{2,1,0:T(8,128)S(1)}, u32[]{:S(2)}, u32[]{:S(2)}) %collective-permute-start.15) | collective-permute-done | bytes 131104 | tf_op jit(solution)/shard_map/ppermute | solution.py:513
  43.9 2.8 %collective-permute-done.16.refs_1_ = f32[2,128,128]{2,1,0:T(8,128)S(1)} collective-permute-done((f32[2,128,128]{2,1,0:T(8,128)S(1)}, f32[2,128,128]{2,1,0:T(8,128)S(1)}, u32[]{:S(2)}, u32[]{:S(2)}) %collective-permute-start.16) | collective-permute-done | bytes 131104 | tf_op jit(solution)/shard_map/ppermute | solution.py:513
  46.7 4.1 %collective-permute-done.17.refs_2_ = f32[2,128,128]{2,1,0:T(8,128)S(1)} collective-permute-done((f32[2,128,128]{2,1,0:T(8,128)S(1)}, f32[2,128,128]{2,1,0:T(8,128)S(1)}, u32[]{:S(2)}, u32[]{:S(2)}) %collective-permute-start.17) | collective-permute-done | bytes 131104 | tf_op jit(solution)/shard_map/ppermute | solution.py:513
  52.0 2.0 %collective-permute-done.18.refs_3_ = f32[2,128,128]{2,1,0:T(8,128)S(1)} collective-permute-done((f32[2,128,128]{2,1,0:T(8,128)S(1)}, f32[2,128,128]{2,1,0:T(8,128)S(1)}, u32[]{:S(2)}, u32[]{:S(2)}) %collective-permute-start.18) | collective-permute-done | bytes 131104 | tf_op jit(solution)/shard_map/ppermute | solution.py:513
  54.0 2.9 %shard_map.65 = (bf16[2,512,512]{2,1,0:T(8,128)(2,1)S(1)}, bf16[2,512,512]{2,1,0:T(8,128)(2,1)S(1)}) custom-call(s32[2]{0:T(128)S(1)} %pad_add_fusion.where, s32[2,512,512]{2,1,0:T(8,128)S(1)} %copy-done), custom_call_target="tpu_custom_call" | custom-call | flops 10485760 | bytes 3145728 | tf_op jit(solution)/shard_map/pallas_call | solution.py:222
  57.1 5.7 %collective-permute-done.4.refs_2_ = f32[2,128,128]{2,1,0:T(8,128)S(1)} collective-permute-done((f32[2,128,128]{2,1,0:T(8,128)S(1)}, f32[2,128,128]{2,1,0:T(8,128)S(1)}, u32[]{:S(2)}, u32[]{:S(2)}) %collective-permute-start.4) | collective-permute-done | bytes 131104 | tf_op jit(solution)/shard_map/ppermute | solution.py:513
  63.3 2.1 %collective-permute-done.6.refs_3_ = f32[2,128,128]{2,1,0:T(8,128)S(1)} collective-permute-done((f32[2,128,128]{2,1,0:T(8,128)S(1)}, f32[2,128,128]{2,1,0:T(8,128)S(1)}, u32[]{:S(2)}, u32[]{:S(2)}) %collective-permute-start.6) | collective-permute-done | bytes 131104 | tf_op jit(solution)/shard_map/ppermute | solution.py:513
  66.0 1.6 %collective-permute-start.3 = (f32[2,128,128]{2,1,0:T(8,128)S(1)}, f32[2,128,128]{2,1,0:T(8,128)S(1)}, u32[]{:S(2)}, u32[]{:S(2)}) collective-permute-start(f32[2,128,128]{2,1,0:T(8,128)S(1)} %collective-permute-done.2.refs_1_), channel_id=1, source_target_pairs={{0,1},{1,0},{2,3},{3,2},{4,5},{5,4},{6,7},{7,6},{8,9},{9,8},{10,11... | collective-permute-start | bytes 393224 | tf_op jit(solution)/shard_map/ppermute | solution.py:526
  67.6 3.0 %shard_map.64 = (bf16[2,512,512]{2,1,0:T(8,128)(2,1)S(1)}, bf16[2,512,512]{2,1,0:T(8,128)(2,1)S(1)}) custom-call(s32[2]{0:T(128)S(1)} %pad_add_fusion.where, s32[2,256,512]{2,1,0:T(8,128)S(1)} %collective-permute-done.19.refs_0_), custom_call_target="tpu_custom_call" | custom-call | flops 10485760 | bytes 3145728 | tf_op jit(solution)/shard_map/pallas_call | solution.py:222
  72.7 4.1 %shard_map.66 = (f32[2,2,512,1024]{3,2,1,0:T(8,128)}, f32[2,512,512]{2,1,0:T(8,128)S(1)}, bf16[2,256,512]{2,1,0:T(8,128)(2,1)S(1)}, bf16[2,256,512]{2,1,0:T(8,128)(2,1)S(1)}) custom-call(bf16[2,256,512]{2,1,0:T(8,128)(2,1)S(1)} %get-tuple-element.55.refs_0_.refs_1_.refs_4_, bf16[2,256,512]{2,1,0:T(8,128)(2,1)S(1)} %get-tuple-element.56.refs_1_.refs_2_.refs_5_, ...), custom_call_target="tpu_custom_call" | custom-call | flops 3221225472 | bytes 4194304 | tf_op jit(solution)/shard_map/pallas_call | solution.py:438
  76.8 5.8 %shard_map.67 = (f32[2,2,512,1024]{3,2,1,0:T(8,128)}, f32[2,512,512]{2,1,0:T(8,128)S(1)}) custom-call(bf16[2,256,512]{2,1,0:T(8,128)(2,1)S(1)} %get-tuple-element.55.refs_0_.refs_1_.refs_4_, bf16[2,256,512]{2,1,0:T(8,128)(2,1)S(1)} %get-tuple-element.56.refs_1_.refs_2_.refs_5_, ...), custom_call_target="tpu_custom_call", output_to_operand_aliasing={{1}: (8, {}), {0}: (9, {})} | custom-call | flops 4026531840 | bytes 4194304 | tf_op jit(solution)/shard_map/pallas_call | solution.py:438
  82.6 2.7 %shard_map.68 = (f32[2,2,512,1024]{3,2,1,0:T(8,128)}, f32[2,512,512]{2,1,0:T(8,128)S(1)}) custom-call(f32[2,128,512]{2,1,0:T(8,128)S(1)} %collective-permute-done.20.refs_0_, bf16[2,256,512]{2,1,0:T(8,128)(2,1)S(1)} %get-tuple-element.55.refs_0_.refs_1_.refs_4_, ...), custom_call_target="tpu_custom_call", output_to_operand_aliasing={{1}: (7, {}), {0}: (8, {})} | custom-call | flops 1610612736 | bytes 4194304 | tf_op jit(solution)/shard_map/pallas_call | solution.py:438
  86.0 1.8 %collective-permute-done.7.refs_3_ = f32[2,128,128]{2,1,0:T(8,128)S(1)} collective-permute-done((f32[2,128,128]{2,1,0:T(8,128)S(1)}, f32[2,128,128]{2,1,0:T(8,128)S(1)}, u32[]{:S(2)}, u32[]{:S(2)}) %collective-permute-start.7) | collective-permute-done | bytes 131104 | tf_op jit(solution)/shard_map/ppermute | solution.py:526
  87.8 3.8 %shard_map.69 = (f32[2,2,512,1024]{3,2,1,0:T(8,128)}, f32[2,256,256]{2,1,0:T(8,128)}) custom-call(f32[2,128,128]{2,1,0:T(8,128)S(1)} %collective-permute-done.1.refs_0_, f32[2,128,128]{2,1,0:T(8,128)S(1)} %collective-permute-done.3.refs_1_, f32[2,128,128]{2,1,0:T(8,128)S(1)} %collective-permute-done.5.refs_2_, ...), custom_call_target="tpu_custom_call", output_to_operand_aliasing={{0}: (11, {})} | custom-call | flops 1610612736 | bytes 4194304 | tf_op jit(solution)/shard_map/pallas_call | solution.py:438
  (46 shorter events, 14.1 us)
Async XLA Ops:
  3.2 62.8 %collective-permute-start.19 = (s32[2,256,512]{2,1,0:T(8,128)}, s32[2,256,512]{2,1,0:T(8,128)S(1)}, u32[]{:S(2)}, u32[]{:S(2)}) collective-permute-start(s32[2,256,512]{2,1,0:T(8,128)} %shard_map.63), channel_id=1, source_target_pairs={{0,1},{1,0},{2,3},{3,2},{4,5},{5,4},{6,7},{7,6},{8,9},{9,8},{10,11... | collective-permute-start | bytes 3145736 | tf_op jit(solution)/shard_map/ppermute | solution.py:505
  5.7 48.4 %copy-start = (s32[2,512,512]{2,1,0:T(8,128)S(1)}, s32[2,512,512]{2,1,0:T(8,128)}, u32[]{:S(2)}) copy-start(s32[2,512,512]{2,1,0:T(8,128)} %refs_0_.1) | copy-start | bytes 6291460
  10.3 6.4 %collective-permute-start.8 = (f32[2,128,128]{2,1,0:T(8,128)S(1)}, f32[2,128,128]{2,1,0:T(8,128)S(1)}, u32[]{:S(2)}, u32[]{:S(2)}) collective-permute-start(f32[2,128,128]{2,1,0:T(8,128)S(1)} %get-tuple-element.45), channel_id=1, source_target_pairs={{0,8},{2,10},{4,12},{6,14},{8,24},{10,26},{12,28},{14,30},{16,0},{... | collective-permute-start | bytes 393224 | tf_op jit(solution)/shard_map/ppermute | solution.py:513
  10.7 6.0 %collective-permute-start.9 = (f32[2,128,128]{2,1,0:T(8,128)S(1)}, f32[2,128,128]{2,1,0:T(8,128)S(1)}, u32[]{:S(2)}, u32[]{:S(2)}) collective-permute-start(f32[2,128,128]{2,1,0:T(8,128)S(1)} %get-tuple-element.46), channel_id=1, source_target_pairs={{0,10},{2,8},{4,14},{6,12},{8,26},{10,24},{12,30},{14,28},{16,2},{... | collective-permute-start | bytes 393224 | tf_op jit(solution)/shard_map/ppermute | solution.py:513
  11.2 8.7 %collective-permute-start.12 = (f32[2,128,128]{2,1,0:T(8,128)S(1)}, f32[2,128,128]{2,1,0:T(8,128)S(1)}, u32[]{:S(2)}, u32[]{:S(2)}) collective-permute-start(f32[2,128,128]{2,1,0:T(8,128)S(1)} %get-tuple-element.50), channel_id=1, source_target_pairs={{0,2},{2,0},{4,6},{6,4},{8,10},{10,8},{12,14},{14,12},{16,18},{18,... | collective-permute-start | bytes 393224 | tf_op jit(solution)/shard_map/ppermute | solution.py:513
  12.4 8.2 %collective-permute-start.13 = (f32[2,128,128]{2,1,0:T(8,128)S(1)}, f32[2,128,128]{2,1,0:T(8,128)S(1)}, u32[]{:S(2)}, u32[]{:S(2)}) collective-permute-start(f32[2,128,128]{2,1,0:T(8,128)S(1)} %get-tuple-element.51), channel_id=1, source_target_pairs={{0,4},{2,6},{4,0},{6,2},{8,12},{10,14},{12,8},{14,10},{16,20},{18,... | collective-permute-start | bytes 393224 | tf_op jit(solution)/shard_map/ppermute | solution.py:513
  16.7 11.4 %collective-permute-start.14 = (f32[2,128,128]{2,1,0:T(8,128)S(1)}, f32[2,128,128]{2,1,0:T(8,128)S(1)}, u32[]{:S(2)}, u32[]{:S(2)}) collective-permute-start(f32[2,128,128]{2,1,0:T(8,128)S(1)} %get-tuple-element.52), channel_id=1, source_target_pairs={{0,6},{2,4},{4,2},{6,0},{8,14},{10,12},{12,10},{14,8},{16,22},{18,... | collective-permute-start | bytes 393224 | tf_op jit(solution)/shard_map/ppermute | solution.py:513
  16.7 11.5 %collective-permute-start.10 = (f32[2,128,128]{2,1,0:T(8,128)S(1)}, f32[2,128,128]{2,1,0:T(8,128)S(1)}, u32[]{:S(2)}, u32[]{:S(2)}) collective-permute-start(f32[2,128,128]{2,1,0:T(8,128)S(1)} %get-tuple-element.47), channel_id=1, source_target_pairs={{0,12},{2,14},{4,8},{6,10},{8,28},{10,30},{12,24},{14,26},{16,4},{... | collective-permute-start | bytes 393224 | tf_op jit(solution)/shard_map/ppermute | solution.py:513
  19.9 12.2 %collective-permute-start.11 = (f32[2,128,128]{2,1,0:T(8,128)S(1)}, f32[2,128,128]{2,1,0:T(8,128)S(1)}, u32[]{:S(2)}, u32[]{:S(2)}) collective-permute-start(f32[2,128,128]{2,1,0:T(8,128)S(1)} %get-tuple-element.48), channel_id=1, source_target_pairs={{0,14},{2,12},{4,10},{6,8},{8,30},{10,28},{12,26},{14,24},{16,6},{... | collective-permute-start | bytes 393224 | tf_op jit(solution)/shard_map/ppermute | solution.py:513
  20.6 16.3 %collective-permute-start = (f32[2,128,128]{2,1,0:T(8,128)S(1)}, f32[2,128,128]{2,1,0:T(8,128)S(1)}, u32[]{:S(2)}, u32[]{:S(2)}) collective-permute-start(f32[2,128,128]{2,1,0:T(8,128)S(1)} %get-tuple-element.41), channel_id=1, source_target_pairs={{0,24},{2,26},{4,28},{6,30},{8,16},{10,18},{12,20},{14,22},{16,8},... | collective-permute-start | bytes 393224 | tf_op jit(solution)/shard_map/ppermute | solution.py:513
  28.1 11.9 %collective-permute-start.2 = (f32[2,128,128]{2,1,0:T(8,128)S(1)}, f32[2,128,128]{2,1,0:T(8,128)S(1)}, u32[]{:S(2)}, u32[]{:S(2)}) collective-permute-start(f32[2,128,128]{2,1,0:T(8,128)S(1)} %get-tuple-element.42), channel_id=1, source_target_pairs={{0,26},{2,24},{4,30},{6,28},{8,18},{10,16},{12,22},{14,20},{16,10}... | collective-permute-start | bytes 393224 | tf_op jit(solution)/shard_map/ppermute | solution.py:513
  32.2 38.4 %collective-permute-start.22 = (f32[2,128,512]{2,1,0:T(8,128)S(1)}, f32[2,128,512]{2,1,0:T(8,128)S(1)}, u32[]{:S(2)}, u32[]{:S(2)}) collective-permute-start(f32[2,128,512]{2,1,0:T(8,128)S(1)} %get-tuple-element.69), channel_id=1, source_target_pairs={{0,1},{1,0},{2,3},{3,2},{4,5},{5,4},{6,7},{7,6},{8,9},{9,8},{10,11... | collective-permute-start | bytes 1572872 | tf_op jit(solution)/shard_map/ppermute | solution.py:523
  32.8 38.4 %collective-permute-start.21 = (f32[2,128,512]{2,1,0:T(8,128)S(1)}, f32[2,128,512]{2,1,0:T(8,128)S(1)}, u32[]{:S(2)}, u32[]{:S(2)}) collective-permute-start(f32[2,128,512]{2,1,0:T(8,128)S(1)} %get-tuple-element.68), channel_id=1, source_target_pairs={{0,1},{1,0},{2,3},{3,2},{4,5},{5,4},{6,7},{7,6},{8,9},{9,8},{10,11... | collective-permute-start | bytes 1572872 | tf_op jit(solution)/shard_map/ppermute | solution.py:523
  37.0 6.9 %collective-permute-start.15 = (f32[2,128,128]{2,1,0:T(8,128)S(1)}, f32[2,128,128]{2,1,0:T(8,128)S(1)}, u32[]{:S(2)}, u32[]{:S(2)}) collective-permute-start(f32[2,128,128]{2,1,0:T(8,128)S(1)} %get-tuple-element.57), channel_id=1, source_target_pairs={{0,16},{2,18},{4,20},{6,22},{8,0},{10,2},{12,4},{14,6},{16,24},{18... | collective-permute-start | bytes 393224 | tf_op jit(solution)/shard_map/ppermute | solution.py:513
  40.0 6.6 %collective-permute-start.16 = (f32[2,128,128]{2,1,0:T(8,128)S(1)}, f32[2,128,128]{2,1,0:T(8,128)S(1)}, u32[]{:S(2)}, u32[]{:S(2)}) collective-permute-start(f32[2,128,128]{2,1,0:T(8,128)S(1)} %get-tuple-element.58), channel_id=1, source_target_pairs={{0,18},{2,16},{4,22},{6,20},{8,2},{10,0},{12,6},{14,4},{16,26},{18... | collective-permute-start | bytes 393224 | tf_op jit(solution)/shard_map/ppermute | solution.py:513
  43.9 6.9 %collective-permute-start.17 = (f32[2,128,128]{2,1,0:T(8,128)S(1)}, f32[2,128,128]{2,1,0:T(8,128)S(1)}, u32[]{:S(2)}, u32[]{:S(2)}) collective-permute-start(f32[2,128,128]{2,1,0:T(8,128)S(1)} %get-tuple-element.59), channel_id=1, source_target_pairs={{0,20},{2,22},{4,16},{6,18},{8,4},{10,6},{12,0},{14,2},{16,28},{18... | collective-permute-start | bytes 393224 | tf_op jit(solution)/shard_map/ppermute | solution.py:513
  46.7 7.4 %collective-permute-start.18 = (f32[2,128,128]{2,1,0:T(8,128)S(1)}, f32[2,128,128]{2,1,0:T(8,128)S(1)}, u32[]{:S(2)}, u32[]{:S(2)}) collective-permute-start(f32[2,128,128]{2,1,0:T(8,128)S(1)} %get-tuple-element.60), channel_id=1, source_target_pairs={{0,22},{2,20},{4,18},{6,16},{8,6},{10,4},{12,2},{14,0},{16,30},{18... | collective-permute-start | bytes 393224 | tf_op jit(solution)/shard_map/ppermute | solution.py:513
  50.8 12.0 %collective-permute-start.4 = (f32[2,128,128]{2,1,0:T(8,128)S(1)}, f32[2,128,128]{2,1,0:T(8,128)S(1)}, u32[]{:S(2)}, u32[]{:S(2)}) collective-permute-start(f32[2,128,128]{2,1,0:T(8,128)S(1)} %get-tuple-element.43), channel_id=1, source_target_pairs={{0,28},{2,30},{4,24},{6,26},{8,20},{10,22},{12,16},{14,18},{16,12}... | collective-permute-start | bytes 393224 | tf_op jit(solution)/shard_map/ppermute | solution.py:513
  54.0 11.3 %collective-permute-start.6 = (f32[2,128,128]{2,1,0:T(8,128)S(1)}, f32[2,128,128]{2,1,0:T(8,128)S(1)}, u32[]{:S(2)}, u32[]{:S(2)}) collective-permute-start(f32[2,128,128]{2,1,0:T(8,128)S(1)} %get-tuple-element.44), channel_id=1, source_target_pairs={{0,30},{2,28},{4,26},{6,24},{8,22},{10,20},{12,18},{14,16},{16,14}... | collective-permute-start | bytes 393224 | tf_op jit(solution)/shard_map/ppermute | solution.py:513
  62.8 19.8 %collective-permute-start.20 = (f32[2,128,512]{2,1,0:T(8,128)S(1)}, f32[2,128,512]{2,1,0:T(8,128)S(1)}, u32[]{:S(2)}, u32[]{:S(2)}) collective-permute-start(f32[2,128,512]{2,1,0:T(8,128)S(1)} %get-tuple-element.67), channel_id=1, source_target_pairs={{0,1},{1,0},{2,3},{3,2},{4,5},{5,4},{6,7},{7,6},{8,9},{9,8},{10,11... | collective-permute-start | bytes 1572872 | tf_op jit(solution)/shard_map/ppermute | solution.py:523
  65.4 20.0 %collective-permute-start.1 = (f32[2,128,128]{2,1,0:T(8,128)S(1)}, f32[2,128,128]{2,1,0:T(8,128)S(1)}, u32[]{:S(2)}, u32[]{:S(2)}) collective-permute-start(f32[2,128,128]{2,1,0:T(8,128)S(1)} %collective-permute-done.refs_0_), channel_id=1, source_target_pairs={{0,1},{1,0},{2,3},{3,2},{4,5},{5,4},{6,7},{7,6},{8,9},{9,8},{10,11... | collective-permute-start | bytes 393224 | tf_op jit(solution)/shard_map/ppermute | solution.py:526
  66.0 19.4 %collective-permute-start.3 = (f32[2,128,128]{2,1,0:T(8,128)S(1)}, f32[2,128,128]{2,1,0:T(8,128)S(1)}, u32[]{:S(2)}, u32[]{:S(2)}) collective-permute-start(f32[2,128,128]{2,1,0:T(8,128)S(1)} %collective-permute-done.2.refs_1_), channel_id=1, source_target_pairs={{0,1},{1,0},{2,3},{3,2},{4,5},{5,4},{6,7},{7,6},{8,9},{9,8},{10,11... | collective-permute-start | bytes 393224 | tf_op jit(solution)/shard_map/ppermute | solution.py:526
  70.6 15.4 %collective-permute-start.5 = (f32[2,128,128]{2,1,0:T(8,128)S(1)}, f32[2,128,128]{2,1,0:T(8,128)S(1)}, u32[]{:S(2)}, u32[]{:S(2)}) collective-permute-start(f32[2,128,128]{2,1,0:T(8,128)S(1)} %collective-permute-done.4.refs_2_), channel_id=1, source_target_pairs={{0,1},{1,0},{2,3},{3,2},{4,5},{5,4},{6,7},{7,6},{8,9},{9,8},{10,11... | collective-permute-start | bytes 393224 | tf_op jit(solution)/shard_map/ppermute | solution.py:526
  71.2 16.6 %collective-permute-start.7 = (f32[2,128,128]{2,1,0:T(8,128)S(1)}, f32[2,128,128]{2,1,0:T(8,128)S(1)}, u32[]{:S(2)}, u32[]{:S(2)}) collective-permute-start(f32[2,128,128]{2,1,0:T(8,128)S(1)} %collective-permute-done.6.refs_3_), channel_id=1, source_target_pairs={{0,1},{1,0},{2,3},{3,2},{4,5},{5,4},{6,7},{7,6},{8,9},{9,8},{10,11... | collective-permute-start | bytes 393224 | tf_op jit(solution)/shard_map/ppermute | solution.py:526
  (3 other events, 9.1 us)

commit v2 on v1

--- a/solution.py
+++ b/solution.py
@@ -410,16 +410,14 @@
         re = q[:beams, :spectra] + q[beams:, spectra:]
         im = q[:beams, spectra:] - q[beams:, :spectra]
         power = (re * re + im * im) * (1.0 / (2 * n * dishes))
-        u_count = spectra // 64
-        got_at = lax.broadcasted_iota(jnp.int32, (spectra, spectra), 0)
-        want_at = lax.broadcasted_iota(jnp.int32, (spectra, spectra), 1)
-        pick = ((got_at % 64) * u_count + got_at // 64 == want_at).astype(bf16)
-        ordered = jnp.zeros_like(power)
-        for _ in range(3):
-            piece = power.astype(bf16)
-            ordered += lax.dot_general(piece, pick, NN, preferred_element_type=f32)
-            power = power - piece.astype(f32)
-        held[p] = ordered
+        lane = lax.broadcasted_iota(jnp.int32, (beams, LANES), 1)
+        for h in range(spectra // LANES):
+            at_lane = lane % 2 * 64 + 32 * h + lane // 4
+            low, high = (
+                jnp.take_along_axis(power[:, i * LANES : (i + 1) * LANES], at_lane, axis=1, mode="promise_in_bounds")
+                for i in range(2)
+            )
+            held[p, :, h * LANES : (h + 1) * LANES] = jnp.where(lane % 4 < 2, low, high)
         copy = pltpu.make_async_copy(held.at[p], q_ref.at[p], held_sems.at[p])
         copy.start()
         copies.append(copy)
@@ -477,7 +475,7 @@
         out_specs=pl.BlockSpec(memory_space=VMEM),
         scratch_shapes=[pltpu.SemaphoreType.DMA((pieces * channels,))],
         out_shape=jax.ShapeDtypeStruct((channels, count, dishes), jnp.int32),
-        compiler_params=pltpu.CompilerParams(vmem_limit_bytes=60 << 20),
+        compiler_params=pltpu.CompilerParams(vmem_limit_bytes=52 << 20),
         cost_estimate=pl.CostEstimate(flops=0, bytes_accessed=2 << 20, transcendentals=0),
     )(phases)
 

time: 91.9 us -> 90.1 us (0.980)
  waiting for transfers between devices: 39.3 us -> 38.1 us
    ppermute x4, waiting for transfers between devices: 2.4 us -> 1.35 us  [whole_step(): raw.append(lax.ppermute(own[k], 'quad', swap))]
    pallas_call x2, Pallas kernels: 5.89 us -> 6.93 us  [gains(): pl.pallas_call(gain_kernel, grid_spec=pltpu.PrefetchScalarGridSpec(num_sc...]
    pallas_call x1, Pallas kernels: 2.5 us -> 1.53 us  [phase_piece(): pl.pallas_call(functools.partial(phase_kernel, beams, first), in_specs=[p...]
  transfers between devices with their start and end apart: 23 -> 23, of which waited for: 13 -> 12; matrix products, arithmetic and copies ran while one was open for 0% -> 0% of each run, Pallas kernels for 26% -> 28%
where the time goes in v2:
time: 90.1 us; the launch traced here: 89.9 us
  waiting for transfers between devices  38.1 us (42%)
  Pallas kernels  29.3 us (33%)
  starting transfers between devices  20.7 us (23%)
  between operations  0.97 us (1%)
    ppermute x15, waiting for transfers between devices, whole_step(): own.append(lax.ppermute(sent[k], 'chan', route) if k else sent[k])  36.8 us
    pallas_call x4, Pallas kernels, products(): pl.pallas_call(kernel, in_specs=[where_it_is if x.shape == vis_shape else...  15.5 us
    ppermute x15, starting transfers between devices, whole_step(): own.append(lax.ppermute(sent[k], 'chan', route) if k else sent[k])  12.3 us
    pallas_call x2, Pallas kernels, gains(): pl.pallas_call(gain_kernel, grid_spec=pltpu.PrefetchScalarGridSpec(num_sc...  6.93 us
    pallas_call x1, Pallas kernels, filter_bank(): pl.pallas_call(functools.partial(filter_kernel, geom), grid_spec=pltpu.Pr...  4.65 us
    ppermute x4, starting transfers between devices, whole_step(): raw.append(lax.ppermute(own[k], 'quad', swap))  4.18 us
    ppermute x3, starting transfers between devices, whole_step(): far.append(lax.ppermute(got[2], 'quad', swap))  2.69 us
  transfers between devices with their start and end apart: 23, of which 12 were waited for; matrix products, arithmetic and copies ran while one was open for 0% of the time, Pallas kernels for 28%

profile of v2, /device:TPU:16, one launch (start us, length us, event | category | flops | bytes accessed | tf_op | source)
XLA Modules:
  0.0 89.9 jit_solution(4318560451042522009)
XLA Ops:
  0.6 1.5 %shard_map.63 = s32[2,256,512]{2,1,0:T(8,128)S(1)} custom-call(s32[2,512,512]{2,1,0:T(8,128)} %refs_0_.1), custom_call_target="tpu_custom_call" | custom-call | bytes 2097152 | tf_op jit(solution)/shard_map/pallas_call | solution.py:472
  2.2 1.6 %collective-permute-start.19 = (s32[2,256,512]{2,1,0:T(8,128)S(1)}, s32[2,256,512]{2,1,0:T(8,128)}, u32[]{:S(2)}, u32[]{:S(2)}) collective-permute-start(s32[2,256,512]{2,1,0:T(8,128)S(1)} %shard_map.63), channel_id=1, source_target_pairs={{0,1},{1,0},{2,3},{3,2},{4,5},{5,4},{6,7},{7,6},{8,9},{9,8},{10,11... | collective-permute-start | bytes 3145736 | tf_op jit(solution)/shard_map/ppermute | solution.py:503
  4.7 4.6 %filter_bank.1 = (f32[2,128,128]{2,1,0:T(8,128)S(1)}, f32[2,128,128]{2,1,0:T(8,128)S(1)}, f32[2,128,128]{2,1,0:T(8,128)S(1)}, f32[2,128,128]{2,1,0:T(8,128)S(1)}...) custom-call(s32[2]{0:T(128)S(1)} %pad_add_fusion.where, ...), custom_call_target="tpu_custom_call" | custom-call | flops 805306368 | bytes 5242880 | tf_op jit(solution)/shard_map/filter_bank/pallas_call | solution.py:177
  12.9 2.8 %collective-permute-done.8.refs_0_ = f32[2,128,128]{2,1,0:T(8,128)S(1)} collective-permute-done((f32[2,128,128]{2,1,0:T(8,128)S(1)}, f32[2,128,128]{2,1,0:T(8,128)S(1)}, u32[]{:S(2)}, u32[]{:S(2)}) %collective-permute-start.8) | collective-permute-done | bytes 131104 | tf_op jit(solution)/shard_map/ppermute | solution.py:511
  15.8 3.2 %collective-permute-start.10 = (f32[2,128,128]{2,1,0:T(8,128)S(1)}, f32[2,128,128]{2,1,0:T(8,128)S(1)}, u32[]{:S(2)}, u32[]{:S(2)}) collective-permute-start(f32[2,128,128]{2,1,0:T(8,128)S(1)} %get-tuple-element.47), channel_id=1, source_target_pairs={{0,12},{2,14},{4,8},{6,10},{8,28},{10,30},{12,24},{14,26},{16,4},{... | collective-permute-start | bytes 393224 | tf_op jit(solution)/shard_map/ppermute | solution.py:511
  19.6 1.8 %collective-permute-start = (f32[2,128,128]{2,1,0:T(8,128)S(1)}, f32[2,128,128]{2,1,0:T(8,128)S(1)}, u32[]{:S(2)}, u32[]{:S(2)}) collective-permute-start(f32[2,128,128]{2,1,0:T(8,128)S(1)} %get-tuple-element.41), channel_id=1, source_target_pairs={{0,24},{2,26},{4,28},{6,30},{8,16},{10,18},{12,20},{14,22},{16,8},... | collective-permute-start | bytes 393224 | tf_op jit(solution)/shard_map/ppermute | solution.py:511
  21.5 5.7 %collective-permute-done.14.refs_3_ = f32[2,128,128]{2,1,0:T(8,128)S(1)} collective-permute-done((f32[2,128,128]{2,1,0:T(8,128)S(1)}, f32[2,128,128]{2,1,0:T(8,128)S(1)}, u32[]{:S(2)}, u32[]{:S(2)}) %collective-permute-start.14) | collective-permute-done | bytes 131104 | tf_op jit(solution)/shard_map/ppermute | solution.py:511
  27.3 3.8 %collective-permute-done.11.refs_3_ = f32[2,128,128]{2,1,0:T(8,128)S(1)} collective-permute-done((f32[2,128,128]{2,1,0:T(8,128)S(1)}, f32[2,128,128]{2,1,0:T(8,128)S(1)}, u32[]{:S(2)}, u32[]{:S(2)}) %collective-permute-start.11) | collective-permute-done | bytes 131104 | tf_op jit(solution)/shard_map/ppermute | solution.py:511
  31.8 1.5 %collective-permute-start.21 = (f32[2,128,512]{2,1,0:T(8,128)S(1)}, f32[2,128,512]{2,1,0:T(8,128)S(1)}, u32[]{:S(2)}, u32[]{:S(2)}) collective-permute-start(f32[2,128,512]{2,1,0:T(8,128)S(1)} %get-tuple-element.68), channel_id=1, source_target_pairs={{0,1},{1,0},{2,3},{3,2},{4,5},{5,4},{6,7},{7,6},{8,9},{9,8},{10,11... | collective-permute-start | bytes 1572872 | tf_op jit(solution)/shard_map/ppermute | solution.py:521
  33.4 2.6 %collective-permute-done.refs_0_ = f32[2,128,128]{2,1,0:T(8,128)S(1)} collective-permute-done((f32[2,128,128]{2,1,0:T(8,128)S(1)}, f32[2,128,128]{2,1,0:T(8,128)S(1)}, u32[]{:S(2)}, u32[]{:S(2)}) %collective-permute-start) | collective-permute-done | bytes 131104 | tf_op jit(solution)/shard_map/ppermute | solution.py:511
  36.0 1.7 %collective-permute-start.15 = (f32[2,128,128]{2,1,0:T(8,128)S(1)}, f32[2,128,128]{2,1,0:T(8,128)S(1)}, u32[]{:S(2)}, u32[]{:S(2)}) collective-permute-start(f32[2,128,128]{2,1,0:T(8,128)S(1)} %get-tuple-element.57), channel_id=1, source_target_pairs={{0,16},{2,18},{4,20},{6,22},{8,0},{10,2},{12,4},{14,6},{16,24},{18... | collective-permute-start | bytes 393224 | tf_op jit(solution)/shard_map/ppermute | solution.py:511
  39.0 3.8 %collective-permute-done.15.refs_0_ = f32[2,128,128]{2,1,0:T(8,128)S(1)} collective-permute-done((f32[2,128,128]{2,1,0:T(8,128)S(1)}, f32[2,128,128]{2,1,0:T(8,128)S(1)}, u32[]{:S(2)}, u32[]{:S(2)}) %collective-permute-start.15) | collective-permute-done | bytes 131104 | tf_op jit(solution)/shard_map/ppermute | solution.py:511
  42.9 2.8 %collective-permute-done.16.refs_1_ = f32[2,128,128]{2,1,0:T(8,128)S(1)} collective-permute-done((f32[2,128,128]{2,1,0:T(8,128)S(1)}, f32[2,128,128]{2,1,0:T(8,128)S(1)}, u32[]{:S(2)}, u32[]{:S(2)}) %collective-permute-start.16) | collective-permute-done | bytes 131104 | tf_op jit(solution)/shard_map/ppermute | solution.py:511
  45.7 4.1 %collective-permute-done.17.refs_2_ = f32[2,128,128]{2,1,0:T(8,128)S(1)} collective-permute-done((f32[2,128,128]{2,1,0:T(8,128)S(1)}, f32[2,128,128]{2,1,0:T(8,128)S(1)}, u32[]{:S(2)}, u32[]{:S(2)}) %collective-permute-start.17) | collective-permute-done | bytes 131104 | tf_op jit(solution)/shard_map/ppermute | solution.py:511
  51.1 2.0 %collective-permute-done.18.refs_3_ = f32[2,128,128]{2,1,0:T(8,128)S(1)} collective-permute-done((f32[2,128,128]{2,1,0:T(8,128)S(1)}, f32[2,128,128]{2,1,0:T(8,128)S(1)}, u32[]{:S(2)}, u32[]{:S(2)}) %collective-permute-start.18) | collective-permute-done | bytes 131104 | tf_op jit(solution)/shard_map/ppermute | solution.py:511
  53.1 2.9 %shard_map.65 = (bf16[2,512,512]{2,1,0:T(8,128)(2,1)S(1)}, bf16[2,512,512]{2,1,0:T(8,128)(2,1)S(1)}) custom-call(s32[2]{0:T(128)S(1)} %pad_add_fusion.where, s32[2,512,512]{2,1,0:T(8,128)S(1)} %copy-done), custom_call_target="tpu_custom_call" | custom-call | flops 10485760 | bytes 3145728 | tf_op jit(solution)/shard_map/pallas_call | solution.py:222
  56.1 5.7 %collective-permute-done.4.refs_2_ = f32[2,128,128]{2,1,0:T(8,128)S(1)} collective-permute-done((f32[2,128,128]{2,1,0:T(8,128)S(1)}, f32[2,128,128]{2,1,0:T(8,128)S(1)}, u32[]{:S(2)}, u32[]{:S(2)}) %collective-permute-start.4) | collective-permute-done | bytes 131104 | tf_op jit(solution)/shard_map/ppermute | solution.py:511
  62.4 2.0 %collective-permute-done.6.refs_3_ = f32[2,128,128]{2,1,0:T(8,128)S(1)} collective-permute-done((f32[2,128,128]{2,1,0:T(8,128)S(1)}, f32[2,128,128]{2,1,0:T(8,128)S(1)}, u32[]{:S(2)}, u32[]{:S(2)}) %collective-permute-start.6) | collective-permute-done | bytes 131104 | tf_op jit(solution)/shard_map/ppermute | solution.py:511
  65.1 1.5 %collective-permute-start.3 = (f32[2,128,128]{2,1,0:T(8,128)S(1)}, f32[2,128,128]{2,1,0:T(8,128)S(1)}, u32[]{:S(2)}, u32[]{:S(2)}) collective-permute-start(f32[2,128,128]{2,1,0:T(8,128)S(1)} %collective-permute-done.2.refs_1_), channel_id=1, source_target_pairs={{0,1},{1,0},{2,3},{3,2},{4,5},{5,4},{6,7},{7,6},{8,9},{9,8},{10,11... | collective-permute-start | bytes 393224 | tf_op jit(solution)/shard_map/ppermute | solution.py:524
  66.6 4.1 %shard_map.64 = (bf16[2,512,512]{2,1,0:T(8,128)(2,1)S(1)}, bf16[2,512,512]{2,1,0:T(8,128)(2,1)S(1)}) custom-call(s32[2]{0:T(128)S(1)} %pad_add_fusion.where, s32[2,256,512]{2,1,0:T(8,128)} %collective-permute-done.19.refs_0_), custom_call_target="tpu_custom_call" | custom-call | flops 10485760 | bytes 3145728 | tf_op jit(solution)/shard_map/pallas_call | solution.py:222
  72.8 4.1 %shard_map.66 = (f32[2,2,512,1024]{3,2,1,0:T(8,128)}, f32[2,512,512]{2,1,0:T(8,128)S(1)}, bf16[2,256,512]{2,1,0:T(8,128)(2,1)S(1)}, bf16[2,256,512]{2,1,0:T(8,128)(2,1)S(1)}) custom-call(bf16[2,256,512]{2,1,0:T(8,128)(2,1)S(1)} %get-tuple-element.55.refs_0_.refs_1_.refs_4_, bf16[2,256,512]{2,1,0:T(8,128)(2,1)S(1)} %get-tuple-element.56.refs_1_.refs_2_.refs_5_, ...), custom_call_target="tpu_custom_call" | custom-call | flops 3221225472 | bytes 4194304 | tf_op jit(solution)/shard_map/pallas_call | solution.py:436
  76.9 5.8 %shard_map.67 = (f32[2,2,512,1024]{3,2,1,0:T(8,128)}, f32[2,512,512]{2,1,0:T(8,128)S(1)}) custom-call(bf16[2,256,512]{2,1,0:T(8,128)(2,1)S(1)} %get-tuple-element.55.refs_0_.refs_1_.refs_4_, bf16[2,256,512]{2,1,0:T(8,128)(2,1)S(1)} %get-tuple-element.56.refs_1_.refs_2_.refs_5_, ...), custom_call_target="tpu_custom_call", output_to_operand_aliasing={{1}: (8, {}), {0}: (9, {})} | custom-call | flops 4026531840 | bytes 4194304 | tf_op jit(solution)/shard_map/pallas_call | solution.py:436
  82.7 2.7 %shard_map.68 = (f32[2,2,512,1024]{3,2,1,0:T(8,128)}, f32[2,512,512]{2,1,0:T(8,128)S(1)}) custom-call(f32[2,128,512]{2,1,0:T(8,128)S(1)} %collective-permute-done.20.refs_0_, bf16[2,256,512]{2,1,0:T(8,128)(2,1)S(1)} %get-tuple-element.55.refs_0_.refs_1_.refs_4_, ...), custom_call_target="tpu_custom_call", output_to_operand_aliasing={{1}: (7, {}), {0}: (8, {})} | custom-call | flops 1610612736 | bytes 4194304 | tf_op jit(solution)/shard_map/pallas_call | solution.py:436
  86.8 2.9 %shard_map.69 = (f32[2,2,512,1024]{3,2,1,0:T(8,128)}, f32[2,256,256]{2,1,0:T(8,128)}) custom-call(f32[2,128,128]{2,1,0:T(8,128)S(1)} %collective-permute-done.1.refs_0_, f32[2,128,128]{2,1,0:T(8,128)S(1)} %collective-permute-done.3.refs_1_, f32[2,128,128]{2,1,0:T(8,128)S(1)} %collective-permute-done.5.refs_2_, ...), custom_call_target="tpu_custom_call", output_to_operand_aliasing={{0}: (11, {})} | custom-call | flops 1610612736 | bytes 4194304 | tf_op jit(solution)/shard_map/pallas_call | solution.py:436
  (46 shorter events, 13.5 us)
Async XLA Ops:
  2.2 62.9 %collective-permute-start.19 = (s32[2,256,512]{2,1,0:T(8,128)S(1)}, s32[2,256,512]{2,1,0:T(8,128)}, u32[]{:S(2)}, u32[]{:S(2)}) collective-permute-start(s32[2,256,512]{2,1,0:T(8,128)S(1)} %shard_map.63), channel_id=1, source_target_pairs={{0,1},{1,0},{2,3},{3,2},{4,5},{5,4},{6,7},{7,6},{8,9},{9,8},{10,11... | collective-permute-start | bytes 3145736 | tf_op jit(solution)/shard_map/ppermute | solution.py:503
  4.7 48.4 %copy-start = (s32[2,512,512]{2,1,0:T(8,128)S(1)}, s32[2,512,512]{2,1,0:T(8,128)}, u32[]{:S(2)}) copy-start(s32[2,512,512]{2,1,0:T(8,128)} %refs_0_.1) | copy-start | bytes 6291460
  9.4 6.4 %collective-permute-start.8 = (f32[2,128,128]{2,1,0:T(8,128)S(1)}, f32[2,128,128]{2,1,0:T(8,128)S(1)}, u32[]{:S(2)}, u32[]{:S(2)}) collective-permute-start(f32[2,128,128]{2,1,0:T(8,128)S(1)} %get-tuple-element.45), channel_id=1, source_target_pairs={{0,8},{2,10},{4,12},{6,14},{8,24},{10,26},{12,28},{14,30},{16,0},{... | collective-permute-start | bytes 393224 | tf_op jit(solution)/shard_map/ppermute | solution.py:511
  9.7 6.0 %collective-permute-start.9 = (f32[2,128,128]{2,1,0:T(8,128)S(1)}, f32[2,128,128]{2,1,0:T(8,128)S(1)}, u32[]{:S(2)}, u32[]{:S(2)}) collective-permute-start(f32[2,128,128]{2,1,0:T(8,128)S(1)} %get-tuple-element.46), channel_id=1, source_target_pairs={{0,10},{2,8},{4,14},{6,12},{8,26},{10,24},{12,30},{14,28},{16,2},{... | collective-permute-start | bytes 393224 | tf_op jit(solution)/shard_map/ppermute | solution.py:511
  10.2 8.7 %collective-permute-start.12 = (f32[2,128,128]{2,1,0:T(8,128)S(1)}, f32[2,128,128]{2,1,0:T(8,128)S(1)}, u32[]{:S(2)}, u32[]{:S(2)}) collective-permute-start(f32[2,128,128]{2,1,0:T(8,128)S(1)} %get-tuple-element.50), channel_id=1, source_target_pairs={{0,2},{2,0},{4,6},{6,4},{8,10},{10,8},{12,14},{14,12},{16,18},{18,... | collective-permute-start | bytes 393224 | tf_op jit(solution)/shard_map/ppermute | solution.py:511
  11.4 8.2 %collective-permute-start.13 = (f32[2,128,128]{2,1,0:T(8,128)S(1)}, f32[2,128,128]{2,1,0:T(8,128)S(1)}, u32[]{:S(2)}, u32[]{:S(2)}) collective-permute-start(f32[2,128,128]{2,1,0:T(8,128)S(1)} %get-tuple-element.51), channel_id=1, source_target_pairs={{0,4},{2,6},{4,0},{6,2},{8,12},{10,14},{12,8},{14,10},{16,20},{18,... | collective-permute-start | bytes 393224 | tf_op jit(solution)/shard_map/ppermute | solution.py:511
  15.8 11.4 %collective-permute-start.14 = (f32[2,128,128]{2,1,0:T(8,128)S(1)}, f32[2,128,128]{2,1,0:T(8,128)S(1)}, u32[]{:S(2)}, u32[]{:S(2)}) collective-permute-start(f32[2,128,128]{2,1,0:T(8,128)S(1)} %get-tuple-element.52), channel_id=1, source_target_pairs={{0,6},{2,4},{4,2},{6,0},{8,14},{10,12},{12,10},{14,8},{16,22},{18,... | collective-permute-start | bytes 393224 | tf_op jit(solution)/shard_map/ppermute | solution.py:511
  15.8 11.5 %collective-permute-start.10 = (f32[2,128,128]{2,1,0:T(8,128)S(1)}, f32[2,128,128]{2,1,0:T(8,128)S(1)}, u32[]{:S(2)}, u32[]{:S(2)}) collective-permute-start(f32[2,128,128]{2,1,0:T(8,128)S(1)} %get-tuple-element.47), channel_id=1, source_target_pairs={{0,12},{2,14},{4,8},{6,10},{8,28},{10,30},{12,24},{14,26},{16,4},{... | collective-permute-start | bytes 393224 | tf_op jit(solution)/shard_map/ppermute | solution.py:511
  18.9 12.2 %collective-permute-start.11 = (f32[2,128,128]{2,1,0:T(8,128)S(1)}, f32[2,128,128]{2,1,0:T(8,128)S(1)}, u32[]{:S(2)}, u32[]{:S(2)}) collective-permute-start(f32[2,128,128]{2,1,0:T(8,128)S(1)} %get-tuple-element.48), channel_id=1, source_target_pairs={{0,14},{2,12},{4,10},{6,8},{8,30},{10,28},{12,26},{14,24},{16,6},{... | collective-permute-start | bytes 393224 | tf_op jit(solution)/shard_map/ppermute | solution.py:511
  19.6 16.3 %collective-permute-start = (f32[2,128,128]{2,1,0:T(8,128)S(1)}, f32[2,128,128]{2,1,0:T(8,128)S(1)}, u32[]{:S(2)}, u32[]{:S(2)}) collective-permute-start(f32[2,128,128]{2,1,0:T(8,128)S(1)} %get-tuple-element.41), channel_id=1, source_target_pairs={{0,24},{2,26},{4,28},{6,30},{8,16},{10,18},{12,20},{14,22},{16,8},... | collective-permute-start | bytes 393224 | tf_op jit(solution)/shard_map/ppermute | solution.py:511
  27.1 11.9 %collective-permute-start.2 = (f32[2,128,128]{2,1,0:T(8,128)S(1)}, f32[2,128,128]{2,1,0:T(8,128)S(1)}, u32[]{:S(2)}, u32[]{:S(2)}) collective-permute-start(f32[2,128,128]{2,1,0:T(8,128)S(1)} %get-tuple-element.42), channel_id=1, source_target_pairs={{0,26},{2,24},{4,30},{6,28},{8,18},{10,16},{12,22},{14,20},{16,10}... | collective-permute-start | bytes 393224 | tf_op jit(solution)/shard_map/ppermute | solution.py:511
  31.3 39.4 %collective-permute-start.22 = (f32[2,128,512]{2,1,0:T(8,128)S(1)}, f32[2,128,512]{2,1,0:T(8,128)S(1)}, u32[]{:S(2)}, u32[]{:S(2)}) collective-permute-start(f32[2,128,512]{2,1,0:T(8,128)S(1)} %get-tuple-element.69), channel_id=1, source_target_pairs={{0,1},{1,0},{2,3},{3,2},{4,5},{5,4},{6,7},{7,6},{8,9},{9,8},{10,11... | collective-permute-start | bytes 1572872 | tf_op jit(solution)/shard_map/ppermute | solution.py:521
  31.8 39.5 %collective-permute-start.21 = (f32[2,128,512]{2,1,0:T(8,128)S(1)}, f32[2,128,512]{2,1,0:T(8,128)S(1)}, u32[]{:S(2)}, u32[]{:S(2)}) collective-permute-start(f32[2,128,512]{2,1,0:T(8,128)S(1)} %get-tuple-element.68), channel_id=1, source_target_pairs={{0,1},{1,0},{2,3},{3,2},{4,5},{5,4},{6,7},{7,6},{8,9},{9,8},{10,11... | collective-permute-start | bytes 1572872 | tf_op jit(solution)/shard_map/ppermute | solution.py:521
  36.0 6.9 %collective-permute-start.15 = (f32[2,128,128]{2,1,0:T(8,128)S(1)}, f32[2,128,128]{2,1,0:T(8,128)S(1)}, u32[]{:S(2)}, u32[]{:S(2)}) collective-permute-start(f32[2,128,128]{2,1,0:T(8,128)S(1)} %get-tuple-element.57), channel_id=1, source_target_pairs={{0,16},{2,18},{4,20},{6,22},{8,0},{10,2},{12,4},{14,6},{16,24},{18... | collective-permute-start | bytes 393224 | tf_op jit(solution)/shard_map/ppermute | solution.py:511
  39.0 6.6 %collective-permute-start.16 = (f32[2,128,128]{2,1,0:T(8,128)S(1)}, f32[2,128,128]{2,1,0:T(8,128)S(1)}, u32[]{:S(2)}, u32[]{:S(2)}) collective-permute-start(f32[2,128,128]{2,1,0:T(8,128)S(1)} %get-tuple-element.58), channel_id=1, source_target_pairs={{0,18},{2,16},{4,22},{6,20},{8,2},{10,0},{12,6},{14,4},{16,26},{18... | collective-permute-start | bytes 393224 | tf_op jit(solution)/shard_map/ppermute | solution.py:511
  42.9 6.9 %collective-permute-start.17 = (f32[2,128,128]{2,1,0:T(8,128)S(1)}, f32[2,128,128]{2,1,0:T(8,128)S(1)}, u32[]{:S(2)}, u32[]{:S(2)}) collective-permute-start(f32[2,128,128]{2,1,0:T(8,128)S(1)} %get-tuple-element.59), channel_id=1, source_target_pairs={{0,20},{2,22},{4,16},{6,18},{8,4},{10,6},{12,0},{14,2},{16,28},{18... | collective-permute-start | bytes 393224 | tf_op jit(solution)/shard_map/ppermute | solution.py:511
  45.7 7.4 %collective-permute-start.18 = (f32[2,128,128]{2,1,0:T(8,128)S(1)}, f32[2,128,128]{2,1,0:T(8,128)S(1)}, u32[]{:S(2)}, u32[]{:S(2)}) collective-permute-start(f32[2,128,128]{2,1,0:T(8,128)S(1)} %get-tuple-element.60), channel_id=1, source_target_pairs={{0,22},{2,20},{4,18},{6,16},{8,6},{10,4},{12,2},{14,0},{16,30},{18... | collective-permute-start | bytes 393224 | tf_op jit(solution)/shard_map/ppermute | solution.py:511
  49.8 12.0 %collective-permute-start.4 = (f32[2,128,128]{2,1,0:T(8,128)S(1)}, f32[2,128,128]{2,1,0:T(8,128)S(1)}, u32[]{:S(2)}, u32[]{:S(2)}) collective-permute-start(f32[2,128,128]{2,1,0:T(8,128)S(1)} %get-tuple-element.43), channel_id=1, source_target_pairs={{0,28},{2,30},{4,24},{6,26},{8,20},{10,22},{12,16},{14,18},{16,12}... | collective-permute-start | bytes 393224 | tf_op jit(solution)/shard_map/ppermute | solution.py:511
  53.1 11.3 %collective-permute-start.6 = (f32[2,128,128]{2,1,0:T(8,128)S(1)}, f32[2,128,128]{2,1,0:T(8,128)S(1)}, u32[]{:S(2)}, u32[]{:S(2)}) collective-permute-start(f32[2,128,128]{2,1,0:T(8,128)S(1)} %get-tuple-element.44), channel_id=1, source_target_pairs={{0,30},{2,28},{4,26},{6,24},{8,22},{10,20},{12,18},{14,16},{16,14}... | collective-permute-start | bytes 393224 | tf_op jit(solution)/shard_map/ppermute | solution.py:511
  61.8 20.9 %collective-permute-start.20 = (f32[2,128,512]{2,1,0:T(8,128)S(1)}, f32[2,128,512]{2,1,0:T(8,128)S(1)}, u32[]{:S(2)}, u32[]{:S(2)}) collective-permute-start(f32[2,128,512]{2,1,0:T(8,128)S(1)} %get-tuple-element.67), channel_id=1, source_target_pairs={{0,1},{1,0},{2,3},{3,2},{4,5},{5,4},{6,7},{7,6},{8,9},{9,8},{10,11... | collective-permute-start | bytes 1572872 | tf_op jit(solution)/shard_map/ppermute | solution.py:521
  64.4 21.0 %collective-permute-start.1 = (f32[2,128,128]{2,1,0:T(8,128)S(1)}, f32[2,128,128]{2,1,0:T(8,128)S(1)}, u32[]{:S(2)}, u32[]{:S(2)}) collective-permute-start(f32[2,128,128]{2,1,0:T(8,128)S(1)} %collective-permute-done.refs_0_), channel_id=1, source_target_pairs={{0,1},{1,0},{2,3},{3,2},{4,5},{5,4},{6,7},{7,6},{8,9},{9,8},{10,11... | collective-permute-start | bytes 393224 | tf_op jit(solution)/shard_map/ppermute | solution.py:524
  65.1 20.3 %collective-permute-start.3 = (f32[2,128,128]{2,1,0:T(8,128)S(1)}, f32[2,128,128]{2,1,0:T(8,128)S(1)}, u32[]{:S(2)}, u32[]{:S(2)}) collective-permute-start(f32[2,128,128]{2,1,0:T(8,128)S(1)} %collective-permute-done.2.refs_1_), channel_id=1, source_target_pairs={{0,1},{1,0},{2,3},{3,2},{4,5},{5,4},{6,7},{7,6},{8,9},{9,8},{10,11... | collective-permute-start | bytes 393224 | tf_op jit(solution)/shard_map/ppermute | solution.py:524
  70.7 14.7 %collective-permute-start.5 = (f32[2,128,128]{2,1,0:T(8,128)S(1)}, f32[2,128,128]{2,1,0:T(8,128)S(1)}, u32[]{:S(2)}, u32[]{:S(2)}) collective-permute-start(f32[2,128,128]{2,1,0:T(8,128)S(1)} %collective-permute-done.4.refs_2_), channel_id=1, source_target_pairs={{0,1},{1,0},{2,3},{3,2},{4,5},{5,4},{6,7},{7,6},{8,9},{9,8},{10,11... | collective-permute-start | bytes 393224 | tf_op jit(solution)/shard_map/ppermute | solution.py:524
  71.4 15.4 %collective-permute-start.7 = (f32[2,128,128]{2,1,0:T(8,128)S(1)}, f32[2,128,128]{2,1,0:T(8,128)S(1)}, u32[]{:S(2)}, u32[]{:S(2)}) collective-permute-start(f32[2,128,128]{2,1,0:T(8,128)S(1)} %collective-permute-done.6.refs_3_), channel_id=1, source_target_pairs={{0,1},{1,0},{2,3},{3,2},{4,5},{5,4},{6,7},{7,6},{8,9},{9,8},{10,11... | collective-permute-start | bytes 393224 | tf_op jit(solution)/shard_map/ppermute | solution.py:524
  (3 other events, 7.2 us)

commit v3 on v2

--- a/solution.py
+++ b/solution.py
@@ -49,15 +49,11 @@
     return np.ascontiguousarray(table.transpose(1, 0, 2, 3)).astype(np.float32)
 
 
-def filter_kernel(geom, where, x_ref, table_ref, taps_ref, *rest):
-    dishes, coarse, sections, rows4, u_count, j_count, spec_rows, row_count, n = geom
-    outs, (coef, coef_hi, coef_lo) = rest[:-3], rest[-3:]
-    me = where[0]
+def coefficients(geom, me, table_ref, coef, coef_hi, coef_lo):
+    sections, rows4, u_count, chunk, n = geom
     size = n // 4
-    chunk = n if coarse == 1 else size
     half = chunk * rows4
-    fine = LANES // u_count
-    phase = lax.broadcasted_iota(jnp.int32, (1, LANES), 1) // fine
+    phase = lax.broadcasted_iota(jnp.int32, (1, LANES), 1) // (LANES // u_count)
     for k in range(n):
         top, kc = k // chunk * u_count * half, k % chunk
         for i in range(2):
@@ -66,6 +62,16 @@
                 row = top + u * half + kc * rows4
                 coef[row : row + rows4, i * LANES : (i + 1) * LANES] = jnp.where(phase == u, base, 0.0)
     coef_hi[...], coef_lo[...] = split(coef[...])
+
+
+def filter_kernel(geom, where, x_ref, coef_hi, coef_lo, taps_ref, *outs):
+    dishes, coarse, sections, rows4, u_count, j_count, spec_rows, row_count, n = geom
+    me = where[0]
+    size = n // 4
+    chunk = n if coarse == 1 else size
+    half = chunk * rows4
+    fine = LANES // u_count
+    phase = lax.broadcasted_iota(jnp.int32, (1, LANES), 1) // fine
 
     taps = [taps_ref[t : t + 1, :] for t in range(2 * u_count)]
     weights = []
@@ -133,7 +139,7 @@
         lax.fori_loop(0, dishes // group, step, 0, unroll=2)
 
 
-def rows_kernel(samples, x_ref, out_ref):
+def rows_kernel(samples, geom, x_ref, table_ref, out_ref, coef_hi, coef_lo, coef):
     full, tail = samples // LANES, samples % LANES
 
     def step(d, carry):
@@ -145,6 +151,7 @@
         return carry
 
     lax.fori_loop(0, x_ref.shape[1], step, 0)
+    coefficients(geom, lax.axis_index("chan"), table_ref, coef, coef_hi, coef_lo)
 
 
 def filter_bank(where, voltages, filter_taps, n):
@@ -159,29 +166,31 @@
     row_count = spec_rows + j_count - 1
     rows4 = per_section * 2
     assert u_count == 4 and taps == 8 and j_count == 3 and spec_rows == 64 and rows4 in (2, 4) and dishes % 4 == 0
-    x = pl.pallas_call(
-        functools.partial(rows_kernel, samples),
-        in_specs=[pl.BlockSpec(memory_space=VMEM)],
-        out_specs=pl.BlockSpec(memory_space=VMEM),
-        out_shape=jax.ShapeDtypeStruct((dishes, coarse, row_count, parts, LANES), f32),
-        compiler_params=pltpu.CompilerParams(vmem_limit_bytes=1 << 20),
+    table = twiddle_table(fine, per_section)
+    rows, width = u_count * n * rows4, 2 * LANES
+    half = jax.ShapeDtypeStruct((rows, width), bf16)
+    chunk = n if coarse == 1 else n // 4
+    x, *coefs = pl.pallas_call(
+        functools.partial(rows_kernel, samples, (sections, rows4, u_count, chunk, n)),
+        in_specs=[pl.BlockSpec(memory_space=VMEM)] * 2,
+        out_specs=[pl.BlockSpec(memory_space=VMEM)] * 3,
+        scratch_shapes=[VMEM((rows, width), f32)],
+        out_shape=[jax.ShapeDtypeStruct((dishes, coarse, row_count, parts, LANES), f32), half, half],
+        compiler_params=pltpu.CompilerParams(vmem_limit_bytes=2 << 20),
         cost_estimate=pl.CostEstimate(flops=0, bytes_accessed=4 << 20, transcendentals=0),
         name="rows",
-    )(voltages)
+    )(voltages, jnp.asarray(table))
     x = x.reshape(dishes * coarse * row_count * parts, LANES)
     taps_rows = jnp.tile(filter_taps, (1, u_count))
     geom = (dishes, coarse, sections, rows4, u_count, j_count, spec_rows, row_count, n)
-    width = 2 * LANES
-    rows = u_count * n * rows4
     block = jax.ShapeDtypeStruct((spectra // LANES, dishes * rows4, LANES), f32)
     return pl.pallas_call(
         functools.partial(filter_kernel, geom),
         grid_spec=pltpu.PrefetchScalarGridSpec(
             num_scalar_prefetch=1,
             grid=(1,),
-            in_specs=[pl.BlockSpec(memory_space=VMEM)] * 3,
+            in_specs=[pl.BlockSpec(memory_space=VMEM)] * 4,
             out_specs=[pl.BlockSpec(memory_space=VMEM)] * n,
-            scratch_shapes=[VMEM((rows, width), f32), VMEM((rows, width), bf16), VMEM((rows, width), bf16)],
         ),
         out_shape=[block] * n,
         compiler_params=pltpu.CompilerParams(vmem_limit_bytes=12 << 20),
@@ -189,7 +198,7 @@
             flops=6 * rows * width * dishes * spec_rows, bytes_accessed=5 << 20, transcendentals=0
         ),
         name="filter_bank",
-    )(where, x, jnp.asarray(twiddle_table(fine, per_section)), taps_rows)
+    )(where, x, *coefs, taps_rows)
 
 
 def gain_kernel(where, *refs):

time: 90.1 us -> 89.5 us (level)
  no operation moved by 1% of the time
where the time goes in v3:
time: 89.5 us; the launch traced here: 89.4 us
  waiting for transfers between devices  38.1 us (43%)
  Pallas kernels  29.4 us (33%)
  starting transfers between devices  20.7 us (23%)
  between operations  0.98 us (1%)
    ppermute x15, waiting for transfers between devices, whole_step(): own.append(lax.ppermute(sent[k], 'chan', route) if k else sent[k])  36.8 us
    pallas_call x4, Pallas kernels, products(): pl.pallas_call(kernel, in_specs=[where_it_is if x.shape == vis_shape else...  15.5 us
    ppermute x15, starting transfers between devices, whole_step(): own.append(lax.ppermute(sent[k], 'chan', route) if k else sent[k])  12.3 us
    pallas_call x2, Pallas kernels, gains(): pl.pallas_call(gain_kernel, grid_spec=pltpu.PrefetchScalarGridSpec(num_sc...  6.93 us
    pallas_call x1, Pallas kernels, filter_bank(): pl.pallas_call(functools.partial(filter_kernel, geom), grid_spec=pltpu.Pr...  4.55 us
    ppermute x4, starting transfers between devices, whole_step(): raw.append(lax.ppermute(own[k], 'quad', swap))  4.18 us
    ppermute x3, starting transfers between devices, whole_step(): far.append(lax.ppermute(got[2], 'quad', swap))  2.72 us
  transfers between devices with their start and end apart: 23, of which 12 were waited for; matrix products, arithmetic and copies ran while one was open for 0% of the time, Pallas kernels for 28%

profile of v3, /device:TPU:16, one launch (start us, length us, event | category | flops | bytes accessed | tf_op | source)
XLA Modules:
  0.0 89.4 jit_solution(9585661192294446817)
XLA Ops:
  0.7 1.5 %shard_map.63 = s32[2,256,512]{2,1,0:T(8,128)S(1)} custom-call(s32[2,512,512]{2,1,0:T(8,128)} %refs_0_.1), custom_call_target="tpu_custom_call" | custom-call | bytes 2097152 | tf_op jit(solution)/shard_map/pallas_call | solution.py:481
  2.2 1.6 %collective-permute-start.19 = (s32[2,256,512]{2,1,0:T(8,128)S(1)}, s32[2,256,512]{2,1,0:T(8,128)}, u32[]{:S(2)}, u32[]{:S(2)}) collective-permute-start(s32[2,256,512]{2,1,0:T(8,128)S(1)} %shard_map.63), channel_id=1, source_target_pairs={{0,1},{1,0},{2,3},{3,2},{4,5},{5,4},{6,7},{7,6},{8,9},{9,8},{10,11... | collective-permute-start | bytes 3145736 | tf_op jit(solution)/shard_map/ppermute | solution.py:512
  4.3 4.5 %filter_bank.1 = (f32[2,128,128]{2,1,0:T(8,128)S(1)}, f32[2,128,128]{2,1,0:T(8,128)S(1)}, f32[2,128,128]{2,1,0:T(8,128)S(1)}, f32[2,128,128]{2,1,0:T(8,128)S(1)}...) custom-call(s32[2]{0:T(128)S(1)} %pad_add_fusion.where, ...), custom_call_target="tpu_custom_call" | custom-call | flops 805306368 | bytes 5242880 | tf_op jit(solution)/shard_map/filter_bank/pallas_call | solution.py:187
  11.0 1.5 %collective-permute-start.13 = (f32[2,128,128]{2,1,0:T(8,128)S(1)}, f32[2,128,128]{2,1,0:T(8,128)S(1)}, u32[]{:S(2)}, u32[]{:S(2)}) collective-permute-start(f32[2,128,128]{2,1,0:T(8,128)S(1)} %get-tuple-element.57), channel_id=1, source_target_pairs={{0,4},{2,6},{4,0},{6,2},{8,12},{10,14},{12,8},{14,10},{16,20},{18,... | collective-permute-start | bytes 393224 | tf_op jit(solution)/shard_map/ppermute | solution.py:520
  12.4 2.8 %collective-permute-done.8.refs_0_ = f32[2,128,128]{2,1,0:T(8,128)S(1)} collective-permute-done((f32[2,128,128]{2,1,0:T(8,128)S(1)}, f32[2,128,128]{2,1,0:T(8,128)S(1)}, u32[]{:S(2)}, u32[]{:S(2)}) %collective-permute-start.8) | collective-permute-done | bytes 131104 | tf_op jit(solution)/shard_map/ppermute | solution.py:520
  15.3 3.2 %collective-permute-start.10 = (f32[2,128,128]{2,1,0:T(8,128)S(1)}, f32[2,128,128]{2,1,0:T(8,128)S(1)}, u32[]{:S(2)}, u32[]{:S(2)}) collective-permute-start(f32[2,128,128]{2,1,0:T(8,128)S(1)} %get-tuple-element.53), channel_id=1, source_target_pairs={{0,12},{2,14},{4,8},{6,10},{8,28},{10,30},{12,24},{14,26},{16,4},{... | collective-permute-start | bytes 393224 | tf_op jit(solution)/shard_map/ppermute | solution.py:520
  19.2 1.8 %collective-permute-start = (f32[2,128,128]{2,1,0:T(8,128)S(1)}, f32[2,128,128]{2,1,0:T(8,128)S(1)}, u32[]{:S(2)}, u32[]{:S(2)}) collective-permute-start(f32[2,128,128]{2,1,0:T(8,128)S(1)} %get-tuple-element.47), channel_id=1, source_target_pairs={{0,24},{2,26},{4,28},{6,30},{8,16},{10,18},{12,20},{14,22},{16,8},... | collective-permute-start | bytes 393224 | tf_op jit(solution)/shard_map/ppermute | solution.py:520
  21.0 5.7 %collective-permute-done.14.refs_3_ = f32[2,128,128]{2,1,0:T(8,128)S(1)} collective-permute-done((f32[2,128,128]{2,1,0:T(8,128)S(1)}, f32[2,128,128]{2,1,0:T(8,128)S(1)}, u32[]{:S(2)}, u32[]{:S(2)}) %collective-permute-start.14) | collective-permute-done | bytes 131104 | tf_op jit(solution)/shard_map/ppermute | solution.py:520
  26.8 3.8 %collective-permute-done.11.refs_3_ = f32[2,128,128]{2,1,0:T(8,128)S(1)} collective-permute-done((f32[2,128,128]{2,1,0:T(8,128)S(1)}, f32[2,128,128]{2,1,0:T(8,128)S(1)}, u32[]{:S(2)}, u32[]{:S(2)}) %collective-permute-start.11) | collective-permute-done | bytes 131104 | tf_op jit(solution)/shard_map/ppermute | solution.py:520
  31.3 1.5 %collective-permute-start.21 = (f32[2,128,512]{2,1,0:T(8,128)S(1)}, f32[2,128,512]{2,1,0:T(8,128)S(1)}, u32[]{:S(2)}, u32[]{:S(2)}) collective-permute-start(f32[2,128,512]{2,1,0:T(8,128)S(1)} %get-tuple-element.74), channel_id=1, source_target_pairs={{0,1},{1,0},{2,3},{3,2},{4,5},{5,4},{6,7},{7,6},{8,9},{9,8},{10,11... | collective-permute-start | bytes 1572872 | tf_op jit(solution)/shard_map/ppermute | solution.py:530
  32.9 2.6 %collective-permute-done.refs_0_ = f32[2,128,128]{2,1,0:T(8,128)S(1)} collective-permute-done((f32[2,128,128]{2,1,0:T(8,128)S(1)}, f32[2,128,128]{2,1,0:T(8,128)S(1)}, u32[]{:S(2)}, u32[]{:S(2)}) %collective-permute-start) | collective-permute-done | bytes 131104 | tf_op jit(solution)/shard_map/ppermute | solution.py:520
  35.5 1.7 %collective-permute-start.15 = (f32[2,128,128]{2,1,0:T(8,128)S(1)}, f32[2,128,128]{2,1,0:T(8,128)S(1)}, u32[]{:S(2)}, u32[]{:S(2)}) collective-permute-start(f32[2,128,128]{2,1,0:T(8,128)S(1)} %get-tuple-element.63), channel_id=1, source_target_pairs={{0,16},{2,18},{4,20},{6,22},{8,0},{10,2},{12,4},{14,6},{16,24},{18... | collective-permute-start | bytes 393224 | tf_op jit(solution)/shard_map/ppermute | solution.py:520
  38.6 3.8 %collective-permute-done.15.refs_0_ = f32[2,128,128]{2,1,0:T(8,128)S(1)} collective-permute-done((f32[2,128,128]{2,1,0:T(8,128)S(1)}, f32[2,128,128]{2,1,0:T(8,128)S(1)}, u32[]{:S(2)}, u32[]{:S(2)}) %collective-permute-start.15) | collective-permute-done | bytes 131104 | tf_op jit(solution)/shard_map/ppermute | solution.py:520
  42.4 2.8 %collective-permute-done.16.refs_1_ = f32[2,128,128]{2,1,0:T(8,128)S(1)} collective-permute-done((f32[2,128,128]{2,1,0:T(8,128)S(1)}, f32[2,128,128]{2,1,0:T(8,128)S(1)}, u32[]{:S(2)}, u32[]{:S(2)}) %collective-permute-start.16) | collective-permute-done | bytes 131104 | tf_op jit(solution)/shard_map/ppermute | solution.py:520
  45.2 4.1 %collective-permute-done.17.refs_2_ = f32[2,128,128]{2,1,0:T(8,128)S(1)} collective-permute-done((f32[2,128,128]{2,1,0:T(8,128)S(1)}, f32[2,128,128]{2,1,0:T(8,128)S(1)}, u32[]{:S(2)}, u32[]{:S(2)}) %collective-permute-start.17) | collective-permute-done | bytes 131104 | tf_op jit(solution)/shard_map/ppermute | solution.py:520
  50.6 2.0 %collective-permute-done.18.refs_3_ = f32[2,128,128]{2,1,0:T(8,128)S(1)} collective-permute-done((f32[2,128,128]{2,1,0:T(8,128)S(1)}, f32[2,128,128]{2,1,0:T(8,128)S(1)}, u32[]{:S(2)}, u32[]{:S(2)}) %collective-permute-start.18) | collective-permute-done | bytes 131104 | tf_op jit(solution)/shard_map/ppermute | solution.py:520
  52.6 2.9 %shard_map.65 = (bf16[2,512,512]{2,1,0:T(8,128)(2,1)S(1)}, bf16[2,512,512]{2,1,0:T(8,128)(2,1)S(1)}) custom-call(s32[2]{0:T(128)S(1)} %pad_add_fusion.where, s32[2,512,512]{2,1,0:T(8,128)S(1)} %copy-done), custom_call_target="tpu_custom_call" | custom-call | flops 10485760 | bytes 3145728 | tf_op jit(solution)/shard_map/pallas_call | solution.py:231
  55.6 5.7 %collective-permute-done.4.refs_2_ = f32[2,128,128]{2,1,0:T(8,128)S(1)} collective-permute-done((f32[2,128,128]{2,1,0:T(8,128)S(1)}, f32[2,128,128]{2,1,0:T(8,128)S(1)}, u32[]{:S(2)}, u32[]{:S(2)}) %collective-permute-start.4) | collective-permute-done | bytes 131104 | tf_op jit(solution)/shard_map/ppermute | solution.py:520
  61.9 2.0 %collective-permute-done.6.refs_3_ = f32[2,128,128]{2,1,0:T(8,128)S(1)} collective-permute-done((f32[2,128,128]{2,1,0:T(8,128)S(1)}, f32[2,128,128]{2,1,0:T(8,128)S(1)}, u32[]{:S(2)}, u32[]{:S(2)}) %collective-permute-start.6) | collective-permute-done | bytes 131104 | tf_op jit(solution)/shard_map/ppermute | solution.py:520
  66.1 4.1 %shard_map.64 = (bf16[2,512,512]{2,1,0:T(8,128)(2,1)S(1)}, bf16[2,512,512]{2,1,0:T(8,128)(2,1)S(1)}) custom-call(s32[2]{0:T(128)S(1)} %pad_add_fusion.where, s32[2,256,512]{2,1,0:T(8,128)} %collective-permute-done.19.refs_0_), custom_call_target="tpu_custom_call" | custom-call | flops 10485760 | bytes 3145728 | tf_op jit(solution)/shard_map/pallas_call | solution.py:231
  72.3 4.1 %shard_map.66 = (f32[2,2,512,1024]{3,2,1,0:T(8,128)}, f32[2,512,512]{2,1,0:T(8,128)S(1)}, bf16[2,256,512]{2,1,0:T(8,128)(2,1)S(1)}, bf16[2,256,512]{2,1,0:T(8,128)(2,1)S(1)}) custom-call(bf16[2,256,512]{2,1,0:T(8,128)(2,1)S(1)} %get-tuple-element.61.refs_0_.refs_1_.refs_4_, bf16[2,256,512]{2,1,0:T(8,128)(2,1)S(1)} %get-tuple-element.62.refs_1_.refs_2_.refs_5_, ...), custom_call_target="tpu_custom_call" | custom-call | flops 3221225472 | bytes 4194304 | tf_op jit(solution)/shard_map/pallas_call | solution.py:445
  76.4 5.8 %shard_map.67 = (f32[2,2,512,1024]{3,2,1,0:T(8,128)}, f32[2,512,512]{2,1,0:T(8,128)S(1)}) custom-call(bf16[2,256,512]{2,1,0:T(8,128)(2,1)S(1)} %get-tuple-element.61.refs_0_.refs_1_.refs_4_, bf16[2,256,512]{2,1,0:T(8,128)(2,1)S(1)} %get-tuple-element.62.refs_1_.refs_2_.refs_5_, ...), custom_call_target="tpu_custom_call", output_to_operand_aliasing={{1}: (8, {}), {0}: (9, {})} | custom-call | flops 4026531840 | bytes 4194304 | tf_op jit(solution)/shard_map/pallas_call | solution.py:445
  82.2 2.7 %shard_map.68 = (f32[2,2,512,1024]{3,2,1,0:T(8,128)}, f32[2,512,512]{2,1,0:T(8,128)S(1)}) custom-call(f32[2,128,512]{2,1,0:T(8,128)S(1)} %collective-permute-done.20.refs_0_, bf16[2,256,512]{2,1,0:T(8,128)(2,1)S(1)} %get-tuple-element.61.refs_0_.refs_1_.refs_4_, ...), custom_call_target="tpu_custom_call", output_to_operand_aliasing={{1}: (7, {}), {0}: (8, {})} | custom-call | flops 1610612736 | bytes 4194304 | tf_op jit(solution)/shard_map/pallas_call | solution.py:445
  86.3 2.9 %shard_map.69 = (f32[2,2,512,1024]{3,2,1,0:T(8,128)}, f32[2,256,256]{2,1,0:T(8,128)}) custom-call(f32[2,128,128]{2,1,0:T(8,128)S(1)} %collective-permute-done.1.refs_0_, f32[2,128,128]{2,1,0:T(8,128)S(1)} %collective-permute-done.3.refs_1_, f32[2,128,128]{2,1,0:T(8,128)S(1)} %collective-permute-done.5.refs_2_, ...), custom_call_target="tpu_custom_call", output_to_operand_aliasing={{0}: (11, {})} | custom-call | flops 1610612736 | bytes 4194304 | tf_op jit(solution)/shard_map/pallas_call | solution.py:445
  (46 shorter events, 13.1 us)
Async XLA Ops:
  2.2 62.5 %collective-permute-start.19 = (s32[2,256,512]{2,1,0:T(8,128)S(1)}, s32[2,256,512]{2,1,0:T(8,128)}, u32[]{:S(2)}, u32[]{:S(2)}) collective-permute-start(s32[2,256,512]{2,1,0:T(8,128)S(1)} %shard_map.63), channel_id=1, source_target_pairs={{0,1},{1,0},{2,3},{3,2},{4,5},{5,4},{6,7},{7,6},{8,9},{9,8},{10,11... | collective-permute-start | bytes 3145736 | tf_op jit(solution)/shard_map/ppermute | solution.py:512
  4.3 48.3 %copy-start = (s32[2,512,512]{2,1,0:T(8,128)S(1)}, s32[2,512,512]{2,1,0:T(8,128)}, u32[]{:S(2)}) copy-start(s32[2,512,512]{2,1,0:T(8,128)} %refs_0_.1) | copy-start | bytes 6291460
  8.9 6.4 %collective-permute-start.8 = (f32[2,128,128]{2,1,0:T(8,128)S(1)}, f32[2,128,128]{2,1,0:T(8,128)S(1)}, u32[]{:S(2)}, u32[]{:S(2)}) collective-permute-start(f32[2,128,128]{2,1,0:T(8,128)S(1)} %get-tuple-element.51), channel_id=1, source_target_pairs={{0,8},{2,10},{4,12},{6,14},{8,24},{10,26},{12,28},{14,30},{16,0},{... | collective-permute-start | bytes 393224 | tf_op jit(solution)/shard_map/ppermute | solution.py:520
  9.3 6.0 %collective-permute-start.9 = (f32[2,128,128]{2,1,0:T(8,128)S(1)}, f32[2,128,128]{2,1,0:T(8,128)S(1)}, u32[]{:S(2)}, u32[]{:S(2)}) collective-permute-start(f32[2,128,128]{2,1,0:T(8,128)S(1)} %get-tuple-element.52), channel_id=1, source_target_pairs={{0,10},{2,8},{4,14},{6,12},{8,26},{10,24},{12,30},{14,28},{16,2},{... | collective-permute-start | bytes 393224 | tf_op jit(solution)/shard_map/ppermute | solution.py:520
  9.7 8.7 %collective-permute-start.12 = (f32[2,128,128]{2,1,0:T(8,128)S(1)}, f32[2,128,128]{2,1,0:T(8,128)S(1)}, u32[]{:S(2)}, u32[]{:S(2)}) collective-permute-start(f32[2,128,128]{2,1,0:T(8,128)S(1)} %get-tuple-element.56), channel_id=1, source_target_pairs={{0,2},{2,0},{4,6},{6,4},{8,10},{10,8},{12,14},{14,12},{16,18},{18,... | collective-permute-start | bytes 393224 | tf_op jit(solution)/shard_map/ppermute | solution.py:520
  11.0 8.2 %collective-permute-start.13 = (f32[2,128,128]{2,1,0:T(8,128)S(1)}, f32[2,128,128]{2,1,0:T(8,128)S(1)}, u32[]{:S(2)}, u32[]{:S(2)}) collective-permute-start(f32[2,128,128]{2,1,0:T(8,128)S(1)} %get-tuple-element.57), channel_id=1, source_target_pairs={{0,4},{2,6},{4,0},{6,2},{8,12},{10,14},{12,8},{14,10},{16,20},{18,... | collective-permute-start | bytes 393224 | tf_op jit(solution)/shard_map/ppermute | solution.py:520
  15.3 11.4 %collective-permute-start.14 = (f32[2,128,128]{2,1,0:T(8,128)S(1)}, f32[2,128,128]{2,1,0:T(8,128)S(1)}, u32[]{:S(2)}, u32[]{:S(2)}) collective-permute-start(f32[2,128,128]{2,1,0:T(8,128)S(1)} %get-tuple-element.58), channel_id=1, source_target_pairs={{0,6},{2,4},{4,2},{6,0},{8,14},{10,12},{12,10},{14,8},{16,22},{18,... | collective-permute-start | bytes 393224 | tf_op jit(solution)/shard_map/ppermute | solution.py:520
  15.3 11.5 %collective-permute-start.10 = (f32[2,128,128]{2,1,0:T(8,128)S(1)}, f32[2,128,128]{2,1,0:T(8,128)S(1)}, u32[]{:S(2)}, u32[]{:S(2)}) collective-permute-start(f32[2,128,128]{2,1,0:T(8,128)S(1)} %get-tuple-element.53), channel_id=1, source_target_pairs={{0,12},{2,14},{4,8},{6,10},{8,28},{10,30},{12,24},{14,26},{16,4},{... | collective-permute-start | bytes 393224 | tf_op jit(solution)/shard_map/ppermute | solution.py:520
  18.5 12.2 %collective-permute-start.11 = (f32[2,128,128]{2,1,0:T(8,128)S(1)}, f32[2,128,128]{2,1,0:T(8,128)S(1)}, u32[]{:S(2)}, u32[]{:S(2)}) collective-permute-start(f32[2,128,128]{2,1,0:T(8,128)S(1)} %get-tuple-element.54), channel_id=1, source_target_pairs={{0,14},{2,12},{4,10},{6,8},{8,30},{10,28},{12,26},{14,24},{16,6},{... | collective-permute-start | bytes 393224 | tf_op jit(solution)/shard_map/ppermute | solution.py:520
  19.2 16.3 %collective-permute-start = (f32[2,128,128]{2,1,0:T(8,128)S(1)}, f32[2,128,128]{2,1,0:T(8,128)S(1)}, u32[]{:S(2)}, u32[]{:S(2)}) collective-permute-start(f32[2,128,128]{2,1,0:T(8,128)S(1)} %get-tuple-element.47), channel_id=1, source_target_pairs={{0,24},{2,26},{4,28},{6,30},{8,16},{10,18},{12,20},{14,22},{16,8},... | collective-permute-start | bytes 393224 | tf_op jit(solution)/shard_map/ppermute | solution.py:520
  26.6 11.9 %collective-permute-start.2 = (f32[2,128,128]{2,1,0:T(8,128)S(1)}, f32[2,128,128]{2,1,0:T(8,128)S(1)}, u32[]{:S(2)}, u32[]{:S(2)}) collective-permute-start(f32[2,128,128]{2,1,0:T(8,128)S(1)} %get-tuple-element.48), channel_id=1, source_target_pairs={{0,26},{2,24},{4,30},{6,28},{8,18},{10,16},{12,22},{14,20},{16,10}... | collective-permute-start | bytes 393224 | tf_op jit(solution)/shard_map/ppermute | solution.py:520
  30.8 39.4 %collective-permute-start.22 = (f32[2,128,512]{2,1,0:T(8,128)S(1)}, f32[2,128,512]{2,1,0:T(8,128)S(1)}, u32[]{:S(2)}, u32[]{:S(2)}) collective-permute-start(f32[2,128,512]{2,1,0:T(8,128)S(1)} %get-tuple-element.75), channel_id=1, source_target_pairs={{0,1},{1,0},{2,3},{3,2},{4,5},{5,4},{6,7},{7,6},{8,9},{9,8},{10,11... | collective-permute-start | bytes 1572872 | tf_op jit(solution)/shard_map/ppermute | solution.py:530
  31.3 39.6 %collective-permute-start.21 = (f32[2,128,512]{2,1,0:T(8,128)S(1)}, f32[2,128,512]{2,1,0:T(8,128)S(1)}, u32[]{:S(2)}, u32[]{:S(2)}) collective-permute-start(f32[2,128,512]{2,1,0:T(8,128)S(1)} %get-tuple-element.74), channel_id=1, source_target_pairs={{0,1},{1,0},{2,3},{3,2},{4,5},{5,4},{6,7},{7,6},{8,9},{9,8},{10,11... | collective-permute-start | bytes 1572872 | tf_op jit(solution)/shard_map/ppermute | solution.py:530
  35.5 6.9 %collective-permute-start.15 = (f32[2,128,128]{2,1,0:T(8,128)S(1)}, f32[2,128,128]{2,1,0:T(8,128)S(1)}, u32[]{:S(2)}, u32[]{:S(2)}) collective-permute-start(f32[2,128,128]{2,1,0:T(8,128)S(1)} %get-tuple-element.63), channel_id=1, source_target_pairs={{0,16},{2,18},{4,20},{6,22},{8,0},{10,2},{12,4},{14,6},{16,24},{18... | collective-permute-start | bytes 393224 | tf_op jit(solution)/shard_map/ppermute | solution.py:520
  38.6 6.6 %collective-permute-start.16 = (f32[2,128,128]{2,1,0:T(8,128)S(1)}, f32[2,128,128]{2,1,0:T(8,128)S(1)}, u32[]{:S(2)}, u32[]{:S(2)}) collective-permute-start(f32[2,128,128]{2,1,0:T(8,128)S(1)} %get-tuple-element.64), channel_id=1, source_target_pairs={{0,18},{2,16},{4,22},{6,20},{8,2},{10,0},{12,6},{14,4},{16,26},{18... | collective-permute-start | bytes 393224 | tf_op jit(solution)/shard_map/ppermute | solution.py:520
  42.4 6.9 %collective-permute-start.17 = (f32[2,128,128]{2,1,0:T(8,128)S(1)}, f32[2,128,128]{2,1,0:T(8,128)S(1)}, u32[]{:S(2)}, u32[]{:S(2)}) collective-permute-start(f32[2,128,128]{2,1,0:T(8,128)S(1)} %get-tuple-element.65), channel_id=1, source_target_pairs={{0,20},{2,22},{4,16},{6,18},{8,4},{10,6},{12,0},{14,2},{16,28},{18... | collective-permute-start | bytes 393224 | tf_op jit(solution)/shard_map/ppermute | solution.py:520
  45.2 7.4 %collective-permute-start.18 = (f32[2,128,128]{2,1,0:T(8,128)S(1)}, f32[2,128,128]{2,1,0:T(8,128)S(1)}, u32[]{:S(2)}, u32[]{:S(2)}) collective-permute-start(f32[2,128,128]{2,1,0:T(8,128)S(1)} %get-tuple-element.66), channel_id=1, source_target_pairs={{0,22},{2,20},{4,18},{6,16},{8,6},{10,4},{12,2},{14,0},{16,30},{18... | collective-permute-start | bytes 393224 | tf_op jit(solution)/shard_map/ppermute | solution.py:520
  49.3 12.0 %collective-permute-start.4 = (f32[2,128,128]{2,1,0:T(8,128)S(1)}, f32[2,128,128]{2,1,0:T(8,128)S(1)}, u32[]{:S(2)}, u32[]{:S(2)}) collective-permute-start(f32[2,128,128]{2,1,0:T(8,128)S(1)} %get-tuple-element.49), channel_id=1, source_target_pairs={{0,28},{2,30},{4,24},{6,26},{8,20},{10,22},{12,16},{14,18},{16,12}... | collective-permute-start | bytes 393224 | tf_op jit(solution)/shard_map/ppermute | solution.py:520
  52.6 11.3 %collective-permute-start.6 = (f32[2,128,128]{2,1,0:T(8,128)S(1)}, f32[2,128,128]{2,1,0:T(8,128)S(1)}, u32[]{:S(2)}, u32[]{:S(2)}) collective-permute-start(f32[2,128,128]{2,1,0:T(8,128)S(1)} %get-tuple-element.50), channel_id=1, source_target_pairs={{0,30},{2,28},{4,26},{6,24},{8,22},{10,20},{12,18},{14,16},{16,14}... | collective-permute-start | bytes 393224 | tf_op jit(solution)/shard_map/ppermute | solution.py:520
  61.3 20.9 %collective-permute-start.20 = (f32[2,128,512]{2,1,0:T(8,128)S(1)}, f32[2,128,512]{2,1,0:T(8,128)S(1)}, u32[]{:S(2)}, u32[]{:S(2)}) collective-permute-start(f32[2,128,512]{2,1,0:T(8,128)S(1)} %get-tuple-element.73), channel_id=1, source_target_pairs={{0,1},{1,0},{2,3},{3,2},{4,5},{5,4},{6,7},{7,6},{8,9},{9,8},{10,11... | collective-permute-start | bytes 1572872 | tf_op jit(solution)/shard_map/ppermute | solution.py:530
  63.9 21.0 %collective-permute-start.1 = (f32[2,128,128]{2,1,0:T(8,128)S(1)}, f32[2,128,128]{2,1,0:T(8,128)S(1)}, u32[]{:S(2)}, u32[]{:S(2)}) collective-permute-start(f32[2,128,128]{2,1,0:T(8,128)S(1)} %collective-permute-done.refs_0_), channel_id=1, source_target_pairs={{0,1},{1,0},{2,3},{3,2},{4,5},{5,4},{6,7},{7,6},{8,9},{9,8},{10,11... | collective-permute-start | bytes 393224 | tf_op jit(solution)/shard_map/ppermute | solution.py:533
  64.7 20.3 %collective-permute-start.3 = (f32[2,128,128]{2,1,0:T(8,128)S(1)}, f32[2,128,128]{2,1,0:T(8,128)S(1)}, u32[]{:S(2)}, u32[]{:S(2)}) collective-permute-start(f32[2,128,128]{2,1,0:T(8,128)S(1)} %collective-permute-done.2.refs_1_), channel_id=1, source_target_pairs={{0,1},{1,0},{2,3},{3,2},{4,5},{5,4},{6,7},{7,6},{8,9},{9,8},{10,11... | collective-permute-start | bytes 393224 | tf_op jit(solution)/shard_map/ppermute | solution.py:533
  70.2 14.7 %collective-permute-start.5 = (f32[2,128,128]{2,1,0:T(8,128)S(1)}, f32[2,128,128]{2,1,0:T(8,128)S(1)}, u32[]{:S(2)}, u32[]{:S(2)}) collective-permute-start(f32[2,128,128]{2,1,0:T(8,128)S(1)} %collective-permute-done.4.refs_2_), channel_id=1, source_target_pairs={{0,1},{1,0},{2,3},{3,2},{4,5},{5,4},{6,7},{7,6},{8,9},{9,8},{10,11... | collective-permute-start | bytes 393224 | tf_op jit(solution)/shard_map/ppermute | solution.py:533
  70.9 15.4 %collective-permute-start.7 = (f32[2,128,128]{2,1,0:T(8,128)S(1)}, f32[2,128,128]{2,1,0:T(8,128)S(1)}, u32[]{:S(2)}, u32[]{:S(2)}) collective-permute-start(f32[2,128,128]{2,1,0:T(8,128)S(1)} %collective-permute-done.6.refs_3_), channel_id=1, source_target_pairs={{0,1},{1,0},{2,3},{3,2},{4,5},{5,4},{6,7},{7,6},{8,9},{9,8},{10,11... | collective-permute-start | bytes 393224 | tf_op jit(solution)/shard_map/ppermute | solution.py:533
  (3 other events, 9.6 us)
